TPU v7x, 32 devices: a whole 2x2x4 slice. The times are simulated.
32 devices in a mesh: lat: 4 (over x, core), lon: 8 (over z, y).
Axes of the slice: x: 2, y: 2, z: 4, core: 2. Of those that a mesh axis runs over, the one named last changes fastest.
Arguments:
- ensemble: bfloat16 [80, 8, 32, 1024], P(None, None, 'lat', 'lon'), may hold values from -6 to 6
- static_sigma: float32 [8], replicated, may hold values from 0.5 to 2
- lat_taps: float32 [17], replicated, may hold values from 0.01 to 0.12
- lon_taps: float32 [17], replicated, may hold values from 0.01 to 0.12
- step_len: float32 [2], replicated, may hold values from 0.2 to 0.6
- send_cols: int32 [4, 8, 32, 256], P('lat', 'lon'), may hold values from 0 to 1023
- send_count: int32 [4, 8, 32], P('lat', 'lon'), may hold values from 128 to 256, as said below
- obs_ref: int32 [4, 8, 4, 2048], P('lat', 'lon'), may hold values from 0 to 8191, as said below
- obs_level: int32 [4, 8, 2048], P('lat', 'lon'), may hold values from 0 to 7
- obs_weight: float32 [4, 8, 4, 2048], P('lat', 'lon'), may hold values from 0 to 1
- innovation: float32 [4, 8, 2048], P('lat', 'lon'), may hold values from -6 to 6
- obs_precision: float32 [4, 8, 2048], P('lat', 'lon'), may hold values from 0.25 to 1
Outputs:
- ens_control: float32 [80, 8, 32, 1024], P(None, None, 'lat', 'lon')
- static_control: float32 [8, 32, 1024], P(None, 'lat', 'lon')
- departures: float32 [4, 8, 2048], P('lat', 'lon')
Inputs may be any that keep to these rules, and one draw needn't show every extreme that they name: `send_count`: number of leading slots of send_cols[a, b, e] that are live. One device receives 256 live slots from every device. `obs_ref`: position in the owning device's list L_e of received live columns; always below the total live slots that device receives.
All inputs are finite; a program needn't handle non-finite values.
Results may differ from a plain program's by a relative error of at most 0.0003.
Values may be sent and summed in bfloat16 or wider, within the bound.
A program may use at most 128 MiB of HBM per device.

v0:
```python
import math

import jax
import jax.numpy as jnp
from jax import lax
from jax.sharding import PartitionSpec as P

HYBRID_STATIC = 0.5
HYBRID_ENSEMBLE = 0.8660254037844386


def padded(block, sides, width):
    for axis, dim in sides:
        count = lax.axis_size(axis)
        forward = [(i, i + 1) for i in range(count - 1)]
        forward.append((count - 1, 0))
        backward = [(target, source) for source, target in forward]
        low = lax.ppermute(
            lax.slice_in_dim(block, block.shape[dim] - width, None, axis=dim), axis, forward
        )
        high = lax.ppermute(lax.slice_in_dim(block, 0, width, axis=dim), axis, backward)
        block = jnp.concatenate([low, block, high], axis=dim)
    return block


def band_matrix(taps, count):
    taps_count = taps.shape[0]
    shape = (count + taps_count - 1, count)
    offset = lax.broadcasted_iota(jnp.int32, shape, 0) - lax.broadcasted_iota(jnp.int32, shape, 1)
    chosen = (offset[:, :, None] == lax.broadcasted_iota(jnp.int32, (1, 1, taps_count), 2)).astype(
        jnp.float32
    )
    return jnp.sum(chosen * taps[None, None, :], axis=2)


def smooth_forward(extended, lat_band, lon_band):
    lat_pass = jnp.einsum("ai,fac->fic", lat_band, extended, precision=lax.Precision.HIGHEST)
    return jnp.einsum("fic,cj->fij", lat_pass, lon_band, precision=lax.Precision.HIGHEST)


def smooth_backward(extended, lat_band, lon_band):
    lon_pass = jnp.einsum("fac,cj->faj", extended, lon_band, precision=lax.Precision.HIGHEST)
    return jnp.einsum("ai,faj->fij", lat_band, lon_pass, precision=lax.Precision.HIGHEST)


def pole_mask(lat_rows, half_width):
    position = lax.broadcasted_iota(jnp.int32, (lat_rows + 2 * half_width, 1), 0)
    band_index = lax.axis_index("lat")
    final_band = lax.axis_size("lat") - 1
    top_rim = jnp.logical_and(position < half_width, band_index == 0)
    bottom_rim = jnp.logical_and(position >= lat_rows + half_width, band_index == final_band)
    return jnp.where(jnp.logical_or(top_rim, bottom_rim), 0.0, 1.0).astype(jnp.float32)


def extend_fields(fields, half_width, pole_keep):
    extended = padded(fields, (("lat", 1), ("lon", 2)), half_width)
    return extended * pole_keep


def route(buffer):
    return lax.all_to_all(buffer, ("lat", "lon"), split_axis=1, concat_axis=1, tiled=True)


def per_device(
    ensemble,
    static_sigma,
    lat_taps,
    lon_taps,
    step_len,
    send_cols,
    send_count,
    obs_ref,
    obs_level,
    obs_weight,
    innovation,
    obs_precision,
):
    members, level_count, lat_rows, lon_cells = ensemble.shape
    half_width = (lat_taps.shape[0] - 1) // 2
    field_count = members * level_count
    ens_scale = HYBRID_ENSEMBLE / math.sqrt(members - 1)
    sigma = static_sigma[:, None, None]
    lat_forward = band_matrix(lat_taps, lat_rows)
    lon_forward = band_matrix(lon_taps, lon_cells)
    lat_reverse = band_matrix(lat_taps[::-1], lat_rows)
    lon_reverse = band_matrix(lon_taps[::-1], lon_cells)
    pole_keep = pole_mask(lat_rows, half_width)
    device_count = send_cols.shape[2]
    slot_count = send_cols.shape[3]
    buffer_size = device_count * slot_count
    column_list = send_cols.reshape(-1)
    received = lax.all_to_all(
        send_count, ("lat", "lon"), split_axis=2, concat_axis=2, tiled=True
    ).reshape(-1)
    slot_ends = jnp.cumsum(received)
    slot_starts = slot_ends - received
    positions = obs_ref.reshape(4, -1)
    source = jnp.sum((positions[:, :, None] >= slot_ends[None, None, :]).astype(jnp.int32), axis=2)
    chosen = (
        source[:, :, None] == lax.broadcasted_iota(jnp.int32, (1, 1, device_count), 2)
    ).astype(jnp.int32)
    first_slot = jnp.sum(chosen * slot_starts[None, None, :], axis=2)
    gather_index = (
        obs_level.reshape(1, -1) * buffer_size + source * slot_count + positions - first_slot
    )
    weights = obs_weight.reshape(4, -1)
    innovations = innovation.reshape(-1)
    precision_obs = obs_precision.reshape(-1)
    member_ext = padded(ensemble, (("lat", 2), ("lon", 3)), half_width) * pole_keep.astype(
        jnp.bfloat16
    )
    control = jnp.zeros(ensemble.shape, jnp.float32)
    static = jnp.zeros((level_count, lat_rows, lon_cells), jnp.float32)
    departure = -innovations
    for iteration in range(step_len.shape[0]):
        if iteration > 0:
            fields = jnp.concatenate(
                [control.reshape(field_count, lat_rows, lon_cells), static], axis=0
            )
            smoothed = smooth_forward(
                extend_fields(fields, half_width, pole_keep), lat_forward, lon_forward
            )
            ens_part = jnp.sum(
                ensemble.astype(jnp.float32) * smoothed[:field_count].reshape(ensemble.shape),
                axis=0,
            )
            increment = ens_scale * ens_part + HYBRID_STATIC * sigma * smoothed[field_count:]
            observe_outgoing = jnp.take(increment.reshape(level_count, -1), column_list, axis=1)
            observe_incoming = route(observe_outgoing)
            picked = jnp.take(observe_incoming.reshape(-1), gather_index)
            departure = jnp.sum(weights * picked, axis=0) - innovations
        incoming = (
            jnp.zeros((level_count * buffer_size,), jnp.float32)
            .at[gather_index.reshape(-1)]
            .add((weights * (precision_obs * departure)[None, :]).reshape(-1))
        )
        outgoing = route(incoming.reshape(level_count, buffer_size))
        forcing = (
            jnp.zeros((level_count, lat_rows * lon_cells), jnp.float32)
            .at[:, column_list]
            .add(outgoing)
        )
        forcing = forcing.reshape(level_count, lat_rows, lon_cells)
        forcing_ext = padded(forcing, (("lat", 1), ("lon", 2)), half_width) * pole_keep
        products = (member_ext.astype(jnp.float32) * forcing_ext[None]).reshape(
            field_count, lat_rows + 2 * half_width, lon_cells + 2 * half_width
        )
        extended = jnp.concatenate([products, forcing_ext], axis=0)
        adjoint = smooth_backward(extended, lat_reverse, lon_reverse)
        control = control - step_len[iteration] * (
            ens_scale * adjoint[:field_count].reshape(ensemble.shape) + control
        )
        static = static - step_len[iteration] * (
            HYBRID_STATIC * sigma * adjoint[field_count:] + static
        )
    return (control, static, departure.reshape(1, 1, -1))


def solution(mesh):
    return jax.shard_map(
        per_device,
        mesh=mesh,
        in_specs=(
            P(None, None, "lat", "lon"),
            P(),
            P(),
            P(),
            P(),
            P("lat", "lon", None, None),
            P("lat", "lon", None),
            P("lat", "lon", None, None),
            P("lat", "lon", None),
            P("lat", "lon", None, None),
            P("lat", "lon", None),
            P("lat", "lon", None),
        ),
        out_specs=(P(None, None, "lat", "lon"), P(None, "lat", "lon"), P("lat", "lon", None)),
        check_vma=False,
    )
```

profile of v0, /device:TPU:0, one launch (start us, length us, event | category | flops | bytes accessed | tf_op | source)
XLA Modules:
  0.0 629.8 jit_solution(9918710402180087394)
XLA Ops:
  4.5 6.6 %all-to-all-start = ((s32[1,1,32]{1,0,2:T(1,128)}), s32[1,1,32]{1,0,2:T(1,128)S(1)}, u32[]{:S(2)}, u32[]{:S(2)}) async-start(s32[1,1,32]{1,0,2:T(1,128)} %copy.195), calls=%async_computation | async-start | bytes 32768 | tf_op jit(solution)/shard_map/all_to_all | solution.py:92
  15.6 19.0 %all-to-all-done = s32[1,1,32]{1,0,2:T(1,128)S(1)} async-done(((s32[1,1,32]{1,0,2:T(1,128)}), s32[1,1,32]{1,0,2:T(1,128)S(1)}, u32[]{:S(2)}, u32[]{:S(2)}) %all-to-all-start) | async-done | bytes 160 | tf_op jit(solution)/shard_map/all_to_all | solution.py:92
  36.3 43.3 %scatter_custom_fusion = f32[65536]{0:T(1024)S(1)} fusion(s32[8192]{0:T(1024)S(1)} %bitcast.159, f32[8192]{0:T(1024)S(1)} %mul.267, f32[]{:T(128)} %constant.22.clone.1), kind=kCustom, calls=%fused_computation.56 | custom fusion | flops 8192 | bytes 262148 | tf_op jit(solution)/shard_map/scatter-add | solution.py:135
  90.5 5.3 all-to-all-done.1
  98.5 44.4 %scatter_custom_fusion.1 = f32[8,1024]{0,1:T(8,128)S(1)} fusion(s32[8192]{0:T(1024)S(1)} %bitcast.145, f32[8192,8]{1,0:T(8,128)} %copy.199, f32[]{:T(128)} %constant.22.clone.1), kind=kCustom, calls=%fused_computation.47 | custom fusion | flops 65536 | bytes 33280 | tf_op jit(solution)/shard_map/scatter-add | solution.py:141
  180.3 6.5 %copy.192 = bf16[80,8,24,8]{3,2,1,0:T(8,128)(2,1)} copy(bf16[80,8,24,8]{0,3,2,1:T(8,128)(2,1)S(1)} %collective-permute-done.2) | data formatting | bytes 491520 | tf_op jit(solution)/shard_map/ppermute | solution.py:18
  186.8 6.5 %copy.194 = bf16[80,8,24,8]{3,2,1,0:T(8,128)(2,1)} copy(bf16[80,8,24,8]{0,3,2,1:T(8,128)(2,1)S(1)} %collective-permute-done.3) | data formatting | bytes 491520 | tf_op jit(solution)/shard_map/ppermute | solution.py:21
  193.3 13.6 %convert_multiply_fusion.1 = f32[640,24,144]{2,1,0:T(8,128)} fusion(f32[8,24,144]{2,1,0:T(8,128)S(1)} %maximum_multiply_fusion.2, bf16[24]{0:T(256)(128)(2,1)S(1)} %get-tuple-element.16, bf16[640,24,8]{2,1,0:T(8,128)(2,1)} %bitcast.118, bf16[640,24,128]{2,1,0:T(8,128)(2,1)} %bitcast.114, bf16[640,24,8]{2,1,0:T(8,128)(2,1)} %bitcast.116), kind=kLoop, calls=%fused_computation.7 | loop fusion | flops 19906560 | bytes 13381680 | tf_op jit(solution)/shard_map/mul | solution.py:145
  206.9 15.9 %fusion = f32[648,24,128]{2,1,0:T(8,128)S(1)} fusion(f32[8,24,144]{2,1,0:T(8,128)S(1)} %maximum_multiply_fusion.2, f32[640,24,144]{2,1,0:T(8,128)} %convert_multiply_fusion.1, f32[144,128]{1,0:T(8,128)S(1)} %get-tuple-element.13), kind=kOutput, calls=%fused_computation.8 | convolution fusion | flops 3442093056 | bytes 16994304 | tf_op jit(solution)/shard_map/fac,cj->faj/dot_general | solution.py:42
  222.9 5.7 fusion.36
  242.9 57.4 %collective-permute-done.8 = f32[648,8,128]{2,1,0:T(8,128)} collective-permute-done((f32[648,8,128]{2,1,0:T(8,128)}, f32[648,8,128]{2,1,0:T(8,128)}, u32[]{:S(2)}, u32[]{:S(2)}) %collective-permute-start.8) | collective-permute-done | bytes 2654240 | tf_op jit(solution)/shard_map/ppermute | solution.py:18
  313.8 21.1 %collective-permute-done.10 = f32[648,24,8]{0,2,1:T(8,128)S(1)} collective-permute-done((f32[648,24,8]{0,2,1:T(8,128)S(1)}, f32[648,24,8]{0,2,1:T(8,128)S(1)}, u32[]{:S(2)}, u32[]{:S(2)}) %collective-permute-start.10) | collective-permute-done | bytes 497696 | tf_op jit(solution)/shard_map/ppermute | solution.py:18
  340.7 13.7 %fusion.11 = f32[648,8,144]{0,1,2:T(8,128)} fusion(f32[648,24,144]{0,2,1:T(8,128)S(1)} %maximum_multiply_fusion, f32[24,8]{0,1:T(8,128)S(1)} %get-tuple-element.14), kind=kOutput, calls=%fused_computation.26 | convolution fusion | flops 214990848 | bytes 11944704 | tf_op jit(solution)/shard_map/ai,fac->fic/dot_general | solution.py:37
  354.4 6.5 %copy.210 = f32[648,8,144]{2,1,0:T(8,128)} copy(f32[648,8,144]{0,1,2:T(8,128)} %fusion.11) | data formatting | bytes 5971968 | tf_op jit(solution)/shard_map/ai,fac->fic/transpose | solution.py:37
  360.9 6.3 %fusion.27 = f32[648,8,128]{2,1,0:T(8,128)S(1)} fusion(f32[648,8,144]{2,1,0:T(8,128)} %copy.210, f32[144,128]{1,0:T(8,128)S(1)} %copy-done.6), kind=kOutput, calls=%fused_computation.63 | convolution fusion | flops 1146617856 | bytes 5713920 | tf_op jit(solution)/shard_map/fic,cj->fij/dot_general | solution.py:38
  372.4 27.7 %gather_fusion = f32[8192,8]{1,0:T(8,128)} fusion(f32[8,1024]{0,1:T(8,128)S(1)} %bitcast.123, s32[8192]{0:T(1024)S(1)} %broadcast_clamp_fusion.1), kind=kCustom, calls=%fused_computation | custom fusion | bytes 557056 | tf_op jit(solution)/shard_map/jit(_take)/gather | solution.py:128
  406.3 10.4 %all-to-all-done.2 = f32[8,32,256]{2,0,1:T(8,128)S(1)} async-done(((f32[8,32,256]{2,0,1:T(8,128)}), f32[8,32,256]{2,0,1:T(8,128)S(1)}, u32[]{:S(2)}, u32[]{:S(2)}) %all-to-all-start.2) | async-done | bytes 262176 | tf_op jit(solution)/shard_map/all_to_all | solution.py:61
  417.0 45.5 %gather_fusion.1 = f32[8192]{0:T(1024)S(1)} fusion(f32[65536]{0:T(1024)S(1)} %bitcast.113, s32[8192]{0:T(1024)S(1)} %broadcast_clamp_fusion), kind=kCustom, calls=%fused_computation.1 | custom fusion | bytes 98304 | tf_op jit(solution)/shard_map/jit(_take)/gather | solution.py:130
  462.7 43.4 %scatter_custom_fusion.2 = f32[65536]{0:T(1024)S(1)} fusion(s32[8192]{0:T(1024)} %bitcast.160, f32[8192]{0:T(1024)S(1)} %mul.301, f32[]{:T(128)} %constant.22.clone.1), kind=kCustom, calls=%fused_computation.54 | custom fusion | flops 8192 | bytes 262656 | tf_op jit(solution)/shard_map/scatter-add | solution.py:135
  506.4 12.7 %all_to_all.35 = f32[8,32,256]{2,0,1:T(8,128)S(1)} all-to-all(f32[8,32,256]{2,0,1:T(8,128)S(1)} %copy.216), channel_id=1, replica_groups=mesh['lat'=4,'lon'=8] {'lat','lon'}, dimensions={1} | all-to-all | bytes 524288 | tf_op jit(solution)/shard_map/all_to_all | solution.py:61
  521.7 44.4 %scatter_custom_fusion.3 = f32[8,1024]{0,1:T(8,128)S(1)} fusion(s32[8192]{0:T(1024)S(1)} %bitcast.147, f32[8192,8]{1,0:T(8,128)} %copy.217, f32[]{:T(128)} %constant.22.clone.1), kind=kCustom, calls=%fused_computation.45 | custom fusion | flops 65536 | bytes 33280 | tf_op jit(solution)/shard_map/scatter-add | solution.py:141
  578.3 13.6 %convert_multiply_fusion = f32[640,24,144]{2,1,0:T(8,128)} fusion(f32[8,24,144]{2,1,0:T(8,128)S(1)} %maximum_multiply_fusion.3, bf16[24]{0:T(256)(128)(2,1)S(1)} %copy-done.21, bf16[640,24,8]{2,1,0:T(8,128)(2,1)} %bitcast.119, bf16[640,24,128]{2,1,0:T(8,128)(2,1)} %bitcast.115, bf16[640,24,8]{2,1,0:T(8,128)(2,1)} %bitcast.117), kind=kLoop, calls=%fused_computation.6 | loop fusion | flops 19906560 | bytes 13381680 | tf_op jit(solution)/shard_map/mul | solution.py:145
  592.0 15.5 %fusion.4 = f32[648,24,128]{2,1,0:T(8,128)S(1)} fusion(f32[8,24,144]{2,1,0:T(8,128)S(1)} %maximum_multiply_fusion.3, f32[640,24,144]{2,1,0:T(8,128)} %convert_multiply_fusion, f32[144,128]{1,0:T(8,128)S(1)} %get-tuple-element.13), kind=kOutput, calls=%fused_computation.12 | convolution fusion | flops 3442093056 | bytes 16994304 | tf_op jit(solution)/shard_map/fac,cj->faj/dot_general | solution.py:42
  607.5 5.7 fusion.34
  (170 shorter events, 136.7 us)
Async XLA Ops:
  0.6 150.7 %collective-permute-start = (bf16[80,8,8,128]{3,2,1,0:T(8,128)(2,1)}, bf16[80,8,8,128]{3,2,1,0:T(8,128)(2,1)}, u32[]{:S(2)}, u32[]{:S(2)}) collective-permute-start(bf16[80,8,8,128]{3,2,1,0:T(8,128)(2,1)} %param.12), channel_id=1, source_target_pairs={{0,8},{8,16},{16,24},{24,0},{1,9},{9,17},{17,25},{25,1},{2,10},{10... | collective-permute-start | bytes 3932168 | tf_op jit(solution)/shard_map/ppermute | solution.py:18
  1.2 152.0 %collective-permute-start.1 = (bf16[80,8,8,128]{3,2,1,0:T(8,128)(2,1)}, bf16[80,8,8,128]{3,2,1,0:T(8,128)(2,1)S(1)}, u32[]{:S(2)}, u32[]{:S(2)}) collective-permute-start(bf16[80,8,8,128]{3,2,1,0:T(8,128)(2,1)} %param.12), channel_id=1, source_target_pairs={{8,0},{16,8},{24,16},{0,24},{9,1},{17,9},{25,17},{1,25},{10,2},{18... | collective-permute-start | bytes 3932168 | tf_op jit(solution)/shard_map/ppermute | solution.py:21
  4.5 30.1 %all-to-all-start = ((s32[1,1,32]{1,0,2:T(1,128)}), s32[1,1,32]{1,0,2:T(1,128)S(1)}, u32[]{:S(2)}, u32[]{:S(2)}) async-start(s32[1,1,32]{1,0,2:T(1,128)} %copy.195), calls=%async_computation | async-start | bytes 32768 | tf_op jit(solution)/shard_map/all_to_all | solution.py:92
  14.2 128.9 %copy-start.10 = (s32[8192,1]{0,1:T(1,128)}, s32[8192,1]{0,1:T(1,128)S(1)}, u32[]{:S(2)}) copy-start(s32[8192,1]{0,1:T(1,128)S(1)} %compare_select_fusion.1) | copy-start | bytes 98308
  36.1 108.7 %copy-start.24 = (f32[2]{0:T(128)S(1)}, f32[2]{0:T(128)}, u32[]{:S(2)}) copy-start(f32[2]{0:T(128)} %param.16) | copy-start | bytes 28
  80.5 15.4 %all-to-all-start.1 = ((f32[8,32,256]{2,0,1:T(8,128)}), f32[8,32,256]{2,0,1:T(8,128)S(1)}, u32[]{:S(2)}, u32[]{:S(2)}) async-start(f32[8,32,256]{2,0,1:T(8,128)} %copy.198), calls=%async_computation.1 | async-start | bytes 524288 | tf_op jit(solution)/shard_map/all_to_all | solution.py:61
  95.9 57.0 %copy-start.3 = (bf16[80,8,8,128]{3,2,1,0:T(8,128)(2,1)S(1)}, bf16[80,8,8,128]{3,2,1,0:T(8,128)(2,1)}, u32[]{:S(2)}) copy-start(bf16[80,8,8,128]{3,2,1,0:T(8,128)(2,1)} %param.12) | copy-start | bytes 3932164
  143.1 3.4 collective-permute-start.4
  143.1 3.3 collective-permute-start.5
  146.6 27.1 %collective-permute-start.6 = (f32[8,24,8]{2,1,0:T(8,128)S(1)}, f32[8,24,8]{2,1,0:T(8,128)S(1)}, u32[]{:S(2)}, u32[]{:S(2)}) collective-permute-start(f32[8,24,8]{2,1,0:T(8,128)S(1)} %get-tuple-element.24), channel_id=1, source_target_pairs={{0,1},{1,2},{2,3},{3,4},{4,5},{5,6},{6,7},{7,0},{8,9},{9,10},{10,1... | collective-permute-start | bytes 18440 | tf_op jit(solution)/shard_map/ppermute | solution.py:18
  147.8 25.9 %collective-permute-start.7 = (f32[8,24,8]{2,1,0:T(8,128)S(1)}, f32[8,24,8]{2,1,0:T(8,128)S(1)}, u32[]{:S(2)}, u32[]{:S(2)}) collective-permute-start(f32[8,24,8]{2,1,0:T(8,128)S(1)} %get-tuple-element.25), channel_id=1, source_target_pairs={{1,0},{2,1},{3,2},{4,3},{5,4},{6,5},{7,6},{0,7},{9,8},{10,9},{11,1... | collective-permute-start | bytes 18440 | tf_op jit(solution)/shard_map/ppermute | solution.py:21
  162.9 17.4 %collective-permute-start.2 = (bf16[80,8,24,8]{0,3,2,1:T(8,128)(2,1)S(1)}, bf16[80,8,24,8]{0,3,2,1:T(8,128)(2,1)S(1)}, u32[]{:S(2)}, u32[]{:S(2)}) collective-permute-start(bf16[80,8,24,8]{0,3,2,1:T(8,128)(2,1)S(1)} %copy.191), channel_id=1, source_target_pairs={{0,1},{1,2},{2,3},{3,4},{4,5},{5,6},{6,7},{7,0},{8,9},{9,10},{10,1... | collective-permute-start | bytes 737288 | tf_op jit(solution)/shard_map/ppermute | solution.py:18
  168.1 18.7 %collective-permute-start.3 = (bf16[80,8,24,8]{0,3,2,1:T(8,128)(2,1)S(1)}, bf16[80,8,24,8]{0,3,2,1:T(8,128)(2,1)S(1)}, u32[]{:S(2)}, u32[]{:S(2)}) collective-permute-start(bf16[80,8,24,8]{0,3,2,1:T(8,128)(2,1)S(1)} %copy.193), channel_id=1, source_target_pairs={{1,0},{2,1},{3,2},{4,3},{5,4},{6,5},{7,6},{0,7},{9,8},{10,9},{11,1... | collective-permute-start | bytes 737288 | tf_op jit(solution)/shard_map/ppermute | solution.py:21
  241.2 59.1 %collective-permute-start.8 = (f32[648,8,128]{2,1,0:T(8,128)}, f32[648,8,128]{2,1,0:T(8,128)}, u32[]{:S(2)}, u32[]{:S(2)}) collective-permute-start(f32[648,8,128]{2,1,0:T(8,128)} %copy.205), channel_id=1, source_target_pairs={{0,8},{8,16},{16,24},{24,0},{1,9},{9,17},{17,25},{25,1},{2,10},{10... | collective-permute-start | bytes 7962632 | tf_op jit(solution)/shard_map/ppermute | solution.py:18
  241.2 62.7 %collective-permute-start.9 = (f32[648,8,128]{2,1,0:T(8,128)}, f32[648,8,128]{2,1,0:T(8,128)}, u32[]{:S(2)}, u32[]{:S(2)}) collective-permute-start(f32[648,8,128]{2,1,0:T(8,128)} %copy.205), channel_id=1, source_target_pairs={{8,0},{16,8},{24,16},{0,24},{9,1},{17,9},{25,17},{1,25},{10,2},{18... | collective-permute-start | bytes 7962632 | tf_op jit(solution)/shard_map/ppermute | solution.py:21
  308.9 25.9 %collective-permute-start.10 = (f32[648,24,8]{0,2,1:T(8,128)S(1)}, f32[648,24,8]{0,2,1:T(8,128)S(1)}, u32[]{:S(2)}, u32[]{:S(2)}) collective-permute-start(f32[648,24,8]{0,2,1:T(8,128)S(1)} %get-tuple-element.18), channel_id=1, source_target_pairs={{0,1},{1,2},{2,3},{3,4},{4,5},{5,6},{6,7},{7,0},{8,9},{9,10},{10,1... | collective-permute-start | bytes 1493000 | tf_op jit(solution)/shard_map/ppermute | solution.py:18
  311.5 25.6 %collective-permute-start.11 = (f32[648,24,8]{0,2,1:T(8,128)S(1)}, f32[648,24,8]{0,2,1:T(8,128)S(1)}, u32[]{:S(2)}, u32[]{:S(2)}) collective-permute-start(f32[648,24,8]{0,2,1:T(8,128)S(1)} %get-tuple-element.19), channel_id=1, source_target_pairs={{1,0},{2,1},{3,2},{4,3},{5,4},{6,5},{7,6},{0,7},{9,8},{10,9},{11,1... | collective-permute-start | bytes 1493000 | tf_op jit(solution)/shard_map/ppermute | solution.py:21
  403.6 13.0 %all-to-all-start.2 = ((f32[8,32,256]{2,0,1:T(8,128)}), f32[8,32,256]{2,0,1:T(8,128)S(1)}, u32[]{:S(2)}, u32[]{:S(2)}) async-start(f32[8,32,256]{2,0,1:T(8,128)} %broadcast_select_fusion), calls=%async_computation.2 | async-start | bytes 524288 | tf_op jit(solution)/shard_map/all_to_all | solution.py:61
  521.7 56.5 %copy-start.19 = (f32[24]{0:T(128)S(1)}, f32[24]{0:T(128)}, u32[]{:S(2)}) copy-start(f32[24]{0:T(128)} %copy-done.17) | copy-start | bytes 292
  521.7 56.7 %copy-start.21 = (bf16[24]{0:T(256)(128)(2,1)S(1)}, bf16[24]{0:T(256)(128)(2,1)}, u32[]{:S(2)}) copy-start(bf16[24]{0:T(256)(128)(2,1)} %copy-done.20) | copy-start | bytes 148
  566.3 3.4 collective-permute-start.12
  566.3 3.3 collective-permute-start.13
  569.7 8.2 %collective-permute-start.14 = (f32[8,24,8]{2,1,0:T(8,128)S(1)}, f32[8,24,8]{2,1,0:T(8,128)S(1)}, u32[]{:S(2)}, u32[]{:S(2)}) collective-permute-start(f32[8,24,8]{2,1,0:T(8,128)S(1)} %get-tuple-element.22), channel_id=1, source_target_pairs={{0,1},{1,2},{2,3},{3,4},{4,5},{5,6},{6,7},{7,0},{8,9},{9,10},{10,1... | collective-permute-start | bytes 18440 | tf_op jit(solution)/shard_map/ppermute | solution.py:18
  571.0 7.2 %collective-permute-start.15 = (f32[8,24,8]{2,1,0:T(8,128)S(1)}, f32[8,24,8]{2,1,0:T(8,128)S(1)}, u32[]{:S(2)}, u32[]{:S(2)}) collective-permute-start(f32[8,24,8]{2,1,0:T(8,128)S(1)} %get-tuple-element.23), channel_id=1, source_target_pairs={{1,0},{2,1},{3,2},{4,3},{5,4},{6,5},{7,6},{0,7},{9,8},{10,9},{11,1... | collective-permute-start | bytes 18440 | tf_op jit(solution)/shard_map/ppermute | solution.py:21
  (20 other events, 426.2 us)
where the time goes:
time: 639 us; the launch traced here: 630 us
  other arithmetic  234 us (37%)
  local copies, waits for them, and re-layouts  153 us (24%)
  waiting for transfers between devices  123 us (19%)
  matrix products  62.8 us (10%)
  starting transfers between devices  41.2 us (6%)
  blocking collectives  12.7 us (2%)
    scatter-add x2, other arithmetic, per_device(): forcing = jnp.zeros((level_count, lat_rows * lon_cells), jnp.float32).at[...  88.9 us
    scatter-add x2, other arithmetic, per_device(): incoming = jnp.zeros((level_count * buffer_size,), jnp.float32).at[gather...  86.7 us
    ppermute x8, waiting for transfers between devices, padded(): lax.ppermute(lax.slice_in_dim(block, block.shape[dim] - width, None, axis...  86.3 us
    gather x2, local copies, waits for them, and re-layouts, per_device(): picked = jnp.take(observe_incoming.reshape(-1), gather_index)  45.6 us
    dot_general x2, matrix products, smooth_backward(): jnp.einsum('fac,cj->faj', extended, lon_band, precision=lax.Precision.HIG...  31.4 us
    gather x2, local copies, waits for them, and re-layouts, per_device(): jnp.take(increment.reshape(level_count, -1), column_list, axis=1)  30.5 us
    mul x2, other arithmetic, per_device(): member_ext.astype(jnp.float32) * forcing_ext[None]  27.2 us
    ppermute x8, starting transfers between devices, padded(): lax.ppermute(lax.slice_in_dim(block, 0, width, axis=dim), axis, backward)  21.5 us
  transfers between devices with their start and end apart: 19, of which 11 were waited for; matrix products, arithmetic and copies ran while one was open for 21% of the time, Pallas kernels for 0%

commit v1 on v0

v1 whole, which is shorter than its diff:
```python
import functools
import math

import jax
import jax.numpy as jnp
from jax import lax
from jax.experimental import pallas as pl
from jax.experimental.pallas import tpu as pltpu
from jax.sharding import PartitionSpec as P

HYBRID_STATIC = 0.5
HYBRID_ENSEMBLE = 0.8660254037844386
BF16 = jnp.bfloat16
F32 = jnp.float32
VMEM = pl.BlockSpec(memory_space=pltpu.VMEM)


def halves(x):
    high = x.astype(BF16)
    return high, (x - high.astype(F32)).astype(BF16)


def dot(a, b):
    return jnp.dot(a, b, preferred_element_type=F32)


def dot_nt(a, b):
    return lax.dot_general(a, b, (((1,), (1,)), ((), ())), preferred_element_type=F32)


def dot3(a, b):
    a_high, a_low = halves(a)
    b_high, b_low = halves(b)
    return dot(a_high, b_high) + dot(a_high, b_low) + dot(a_low, b_high)


def iota(shape, dim):
    return lax.broadcasted_iota(jnp.int32, shape, dim)


def obs_kernel(picking, chunk, *refs):
    if picking:
        table, hi, lo, weight, innov, prec, departure, out = refs
        table_high, table_low = halves(table[...])
    else:
        hi, lo, weight, innov, prec, departure, out = refs
    rows, slots = out.shape
    points = hi.shape[0]
    out[...] = jnp.zeros_like(out)

    def step(index, carry):
        where = pl.ds(pl.multiple_of(index * chunk, chunk), chunk)
        row_ids = iota((rows, chunk), 0)
        slot_ids = iota((slots, chunk), 0)
        value = -innov[:, where]
        if picking:
            for q in range(points):
                lo_hot = jnp.where(slot_ids == lo[q : q + 1, where], 1.0, 0.0).astype(BF16)
                product = dot(table_high, lo_hot) + dot(table_low, lo_hot)
                picked = jnp.sum(
                    jnp.where(row_ids == hi[q : q + 1, where], product, 0.0), axis=0, keepdims=True
                )
                value = value + weight[q : q + 1, where] * picked
        departure[:, where] = value
        value = prec[:, where] * value
        total = None
        for q in range(points):
            lo_hot = jnp.where(slot_ids == lo[q : q + 1, where], 1.0, 0.0).astype(BF16)
            pushed = weight[q : q + 1, where] * value
            high = pushed.astype(BF16).astype(F32)
            chosen = row_ids == hi[q : q + 1, where]
            term = dot_nt(jnp.where(chosen, high, 0.0).astype(BF16), lo_hot) + dot_nt(
                jnp.where(chosen, pushed - high, 0.0).astype(BF16), lo_hot
            )
            total = term if total is None else total + term
        out[...] += total
        return carry

    lax.fori_loop(0, hi.shape[1] // chunk, step, 0)


def observe(table, hi, lo, weight, innov, prec, rows, slots):
    operands = (hi, lo, weight, innov, prec)
    if table is not None:
        operands = (table,) + operands
    chunk = 512 if rows <= 256 else 256
    return pl.pallas_call(
        functools.partial(obs_kernel, table is not None, chunk),
        out_shape=(
            jax.ShapeDtypeStruct(innov.shape, F32),
            jax.ShapeDtypeStruct((rows, slots), F32),
        ),
        in_specs=[VMEM] * len(operands),
        out_specs=(VMEM, VMEM),
        name="observe",
    )(*operands)


def slots_kernel(cols, field, out):
    cells = field.shape[1]
    levels, width = out.shape[1:]
    lat_rows = field.shape[0] // levels
    both = jnp.concatenate(halves(field[...]), axis=0)

    def step(index, carry):
        col = cols[pl.ds(index, 1), :]
        cell_hot = jnp.where(iota((cells, width), 0) == col % cells, 1.0, 0.0).astype(BF16)
        product = dot(both, cell_hot)
        product = product[: field.shape[0]] + product[field.shape[0] :]
        row = jnp.broadcast_to(col // cells, (levels, width))
        total = jnp.zeros((levels, width), F32)
        for r in range(lat_rows):
            total = jnp.where(row == r, product[r * levels : (r + 1) * levels], total)
        out[index] = total
        return carry

    lax.fori_loop(0, cols.shape[0], step, 0, unroll=2)


def columns_kernel(cols, values, out):
    cells = out.shape[1]
    levels, width = values.shape[1:]
    lat_rows = out.shape[0] // levels

    def step(index, total):
        col = cols[pl.ds(index, 1), :]
        cell_hot = jnp.where(iota((cells, width), 0) == col % cells, 1.0, 0.0).astype(BF16)
        row = jnp.broadcast_to(col // cells, (levels, width))
        value = values[index]
        high = value.astype(BF16).astype(F32)
        parts = [jnp.where(row == r, high, 0.0) for r in range(lat_rows)]
        parts += [jnp.where(row == r, value - high, 0.0) for r in range(lat_rows)]
        return total + dot_nt(jnp.concatenate(parts, axis=0).astype(BF16), cell_hot)

    total = lax.fori_loop(
        0, cols.shape[0], step, jnp.zeros((2 * out.shape[0], cells), F32), unroll=2
    )
    out[...] = total[: out.shape[0]] + total[out.shape[0] :]


def covariance_kernel(blocks_lat, blocks_lon, coef, members, forcing, lat_op, lon_op, out, wide, mid):
    count = members.shape[1]
    rows, cells = forcing.shape[1:]
    height = blocks_lat * rows
    fields = count + 1
    for b in range(blocks_lon):
        for a in range(blocks_lat):
            spot = a * blocks_lon + b
            part = forcing[spot]
            for k in range(fields):
                piece = part if k == count else members[spot, k].astype(F32) * part
                at = pl.ds(k * height + a * rows, rows)
                wide[at, (b + 1) * cells : (b + 2) * cells] = piece
                if b == 0:
                    wide[at, (blocks_lon + 1) * cells :] = piece
                if b == blocks_lon - 1:
                    wide[at, :cells] = piece
    lon_high, lon_low = halves(lon_op[...])
    for b in range(blocks_lon):
        high, low = halves(wide[:, b * cells : (b + 3) * cells])
        mid[:, b * cells : (b + 1) * cells] = (
            dot(high, lon_high) + dot(high, lon_low) + dot(low, lon_high)
        )
    size = lat_op.shape[0]
    group = size // height
    for first in range(0, fields, group):
        where = pl.ds(first * height, size)
        wide[where, : blocks_lon * cells] = dot3(lat_op[...], mid[where, :])
    for a in range(blocks_lat):
        for b in range(blocks_lon):
            spot = a * blocks_lon + b
            total = coef[0] * wide[
                pl.ds(count * height + a * rows, rows), b * cells : (b + 1) * cells
            ]
            for k in range(count):
                total = total + coef[1] * (
                    members[spot, k].astype(F32)
                    * wide[pl.ds(k * height + a * rows, rows), b * cells : (b + 1) * cells]
                )
            out[spot] = total


def adjoint_kernel(scale, members, edges, field, sigma, lon_op, lat_op, out, static_out):
    batch, levels, rows, cells = out.shape
    lon_high, lon_low = halves(lon_op[...])

    def smooth(pieces, count):
        passes = []
        for piece in pieces:
            high, low = halves(piece)
            passes.append(
                (dot(high, lon_high) + dot(high, lon_low) + dot(low, lon_high)).reshape(
                    count, rows, cells
                )
            )
        stacked = jnp.concatenate(passes, axis=1)
        group = lat_op.shape[0] // rows
        results = []
        for first in range(0, count, group):
            results.append(
                dot3(
                    lat_op[...],
                    stacked[first : first + group].reshape(group * 3 * rows, cells),
                )
            )
        return jnp.concatenate(results, axis=0)

    count = batch * levels
    pieces = []
    for part in range(3):
        block = members[part].astype(F32) * field[part, :, :, :cells][None]
        edge = edges[part].astype(F32) * field[part, :, :, cells:][None]
        pieces.append(jnp.concatenate([block, edge], axis=-1).reshape(count * rows, 2 * cells))
    out[...] = scale * smooth(pieces, count).reshape(out.shape)

    @pl.when(pl.program_id(0) == 0)
    def _():
        pieces = [field[part].reshape(levels * rows, 2 * cells) for part in range(3)]
        static_out[...] = sigma[...] * smooth(pieces, levels).reshape(static_out.shape)


def shift(block, axis, step):
    count = lax.axis_size(axis)
    return lax.ppermute(block, axis, [(i, (i + step) % count) for i in range(count)])


def toeplitz(taps, shape, centre):
    offset = iota(shape, 0) - iota(shape, 1) + centre
    return jnp.sum(
        jnp.where(offset[:, :, None] == iota((1, 1, taps.shape[0]), 2), taps[None, None, :], 0.0),
        axis=2,
    )


def block_diagonal(matrix, count):
    rows, cols = matrix.shape
    tiled = jnp.tile(matrix, (count, count))
    return jnp.where(iota(tiled.shape, 0) // rows == iota(tiled.shape, 1) // cols, tiled, 0.0)


def divisor(count, limit):
    return max(n for n in range(1, count + 1) if count % n == 0 and (n <= limit or n == 1))


def per_device(
    ensemble,
    static_sigma,
    lat_taps,
    lon_taps,
    step_len,
    send_cols,
    send_count,
    obs_ref,
    obs_level,
    obs_weight,
    innovation,
    obs_precision,
):
    members, levels, rows, cells = ensemble.shape
    half = (lat_taps.shape[0] - 1) // 2
    n_lat, n_lon = lax.axis_size("lat"), lax.axis_size("lon")
    devices = n_lat * n_lon
    slots = send_cols.shape[3]
    both = ("lat", "lon")
    scale = HYBRID_ENSEMBLE / math.sqrt(members - 1)
    lat_at = lax.axis_index("lat")
    lon_at = lax.axis_index("lon")

    received = lax.all_to_all(send_count, both, split_axis=2, concat_axis=2, tiled=True).reshape(-1)
    ends = jnp.cumsum(received)
    starts = ends - received
    positions = obs_ref.reshape(obs_ref.shape[2], -1)
    past = positions[:, :, None] >= ends[None, None, :]
    source = jnp.sum(past.astype(jnp.int32), axis=2)
    lo = positions - jnp.sum(jnp.where(past, received[None, None, :], 0), axis=2)
    hi = source * levels + obs_level.reshape(1, -1)
    weight = obs_weight.reshape(positions.shape)
    innov = innovation.reshape(1, -1)
    prec = obs_precision.reshape(1, -1)

    groups = devices // levels
    per_group = members // groups
    device_at = lat_at * n_lon + lon_at
    level_at = device_at % levels
    spread = (
        ensemble.reshape(groups, per_group, levels, rows, cells)
        .transpose(0, 2, 1, 3, 4)
        .reshape(devices, per_group, rows, cells)
    )
    whole = lax.all_to_all(spread, both, split_axis=0, concat_axis=0, tiled=True)

    pick = jnp.concatenate(
        [
            (iota((half, cells), 1) == iota((half, cells), 0) + cells - half),
            (iota((half, cells), 1) == iota((half, cells), 0)),
        ],
        axis=0,
    ).astype(BF16)
    sides = lax.dot_general(
        pick,
        ensemble.reshape(-1, cells),
        (((1,), (1,)), ((), ())),
        preferred_element_type=BF16,
    )
    sides = jnp.concatenate([shift(sides[:half], "lon", 1), shift(sides[half:], "lon", -1)], axis=0)
    block3 = jnp.stack([shift(ensemble, "lat", 1), ensemble, shift(ensemble, "lat", -1)])
    sides3 = jnp.stack([shift(sides, "lat", 1), sides, shift(sides, "lat", -1)])
    place = (iota((2 * half, cells), 0) == iota((2 * half, cells), 1)).astype(BF16)
    edges3 = lax.dot_general(
        sides3, place, (((1,), (0,)), ((), ())), preferred_element_type=BF16
    ).reshape(block3.shape)

    whole_lat = toeplitz(lat_taps, (n_lat * rows, n_lat * rows), half).T
    lat_cov = jnp.dot(whole_lat, whole_lat.T, precision=lax.Precision.HIGHEST)
    lat_cov = block_diagonal(
        lat_cov, divisor(per_group + 1, max(1, 256 // (n_lat * rows)))
    )
    lon_corr = jnp.sum(
        jnp.where(
            iota((4 * half + 1, lon_taps.shape[0], lon_taps.shape[0]), 1)
            - iota((4 * half + 1, lon_taps.shape[0], lon_taps.shape[0]), 2)
            + 2 * half
            == iota((4 * half + 1, lon_taps.shape[0], lon_taps.shape[0]), 0),
            lon_taps[None, :, None] * lon_taps[None, None, :],
            0.0,
        ),
        axis=(1, 2),
    )
    lon_cov = toeplitz(lon_corr, (3 * cells, cells), 2 * half - cells)
    reverse = lon_taps[::-1]
    extended = toeplitz(reverse, (cells + 2 * half, cells), 0)
    lon_adjoint = jnp.concatenate(
        [
            extended[half : half + cells],
            extended[:half],
            extended[half + cells :],
            jnp.zeros((cells - 2 * half, cells), F32),
        ],
        axis=0,
    )
    lat_adjoint = block_diagonal(
        toeplitz(lat_taps[::-1], (rows + 2 * half, rows), 0).T, levels
    )

    wide_slots = max(slots, 256)
    cols = send_cols.reshape(-1, wide_slots)
    per_row = wide_slots // slots

    def to_buffer(packed):
        if per_row == 1:
            return packed
        return (
            packed.reshape(-1, levels, per_row, slots)
            .transpose(0, 2, 1, 3)
            .reshape(devices, levels, slots)
        )

    def from_buffer(buffer):
        if per_row == 1:
            return buffer
        return (
            buffer.reshape(-1, per_row, levels, slots)
            .transpose(0, 2, 1, 3)
            .reshape(-1, levels, wide_slots)
        )

    def route(buffer):
        return lax.all_to_all(buffer, both, split_axis=0, concat_axis=0, tiled=True)

    held = jnp.zeros((levels, rows, cells), F32)
    table = None
    for iteration in range(step_len.shape[0]):
        if iteration > 0:
            sent = jnp.broadcast_to(held[None], (groups,) + held.shape).reshape(
                devices, rows, cells
            )
            field = route(sent)
            static_coef = jnp.where(
                device_at < levels, HYBRID_STATIC**2 * static_sigma[level_at] ** 2, 0.0
            )
            coef = jnp.stack([static_coef, jnp.full((), scale * scale, F32)])
            height = n_lat * rows
            fields = per_group + 1
            part = pl.pallas_call(
                functools.partial(covariance_kernel, n_lat, n_lon),
                out_shape=jax.ShapeDtypeStruct((devices, rows, cells), F32),
                in_specs=[pl.BlockSpec(memory_space=pltpu.SMEM)] + [VMEM] * 4,
                out_specs=VMEM,
                scratch_shapes=[
                    pltpu.VMEM((fields * height, (n_lon + 2) * cells), F32),
                    pltpu.VMEM((fields * height, n_lon * cells), F32),
                ],
                name="covariance",
            )(coef, whole, field, lat_cov, lon_cov)
            increment = jnp.sum(
                route(part).reshape(groups, levels, rows, cells), axis=0
            )
            packed = pl.pallas_call(
                slots_kernel,
                out_shape=jax.ShapeDtypeStruct((cols.shape[0], levels, wide_slots), F32),
                in_specs=[VMEM, VMEM],
                out_specs=VMEM,
                name="to_slots",
            )(cols, increment.transpose(1, 0, 2).reshape(rows * levels, cells))
            table = route(to_buffer(packed)).reshape(devices * levels, slots)
        departure, pushed = observe(
            table, hi, lo, weight, innov, prec, devices * levels, slots
        )
        incoming = from_buffer(route(pushed.reshape(devices, levels, slots)))
        forcing = pl.pallas_call(
            columns_kernel,
            out_shape=jax.ShapeDtypeStruct((rows * levels, cells), F32),
            in_specs=[VMEM, VMEM],
            out_specs=VMEM,
            name="to_columns",
        )(cols, incoming)
        forcing = forcing.reshape(rows, levels, cells).transpose(1, 0, 2)
        held = held - step_len[iteration] * (forcing + held)

    low = shift(held[:, :, cells - half :], "lon", 1)
    high = shift(held[:, :, :half], "lon", -1)
    wide = jnp.concatenate(
        [held, low, high, jnp.zeros((levels, rows, cells - 2 * half), F32)], axis=2
    )
    above = jnp.where(lat_at > 0, shift(wide, "lat", 1), 0.0)
    below = jnp.where(lat_at < n_lat - 1, shift(wide, "lat", -1), 0.0)
    wide3 = jnp.stack([above, wide, below])
    batch = divisor(members, 8)
    sigma = jnp.broadcast_to(
        (HYBRID_STATIC * static_sigma)[:, None, None], (levels, rows, cells)
    )
    member_spec = pl.BlockSpec((3, batch, levels, rows, cells), lambda k: (0, k, 0, 0, 0))
    control, static = pl.pallas_call(
        functools.partial(adjoint_kernel, scale),
        grid=(members // batch,),
        out_shape=(
            jax.ShapeDtypeStruct(ensemble.shape, F32),
            jax.ShapeDtypeStruct((levels, rows, cells), F32),
        ),
        in_specs=[member_spec, member_spec] + [VMEM] * 4,
        out_specs=(
            pl.BlockSpec((batch, levels, rows, cells), lambda k: (k, 0, 0, 0)),
            pl.BlockSpec((levels, rows, cells), lambda k: (0, 0, 0)),
        ),
        name="adjoint",
    )(block3, edges3, wide3, sigma, lon_adjoint, lat_adjoint)
    return control, static, departure.reshape(1, 1, -1)


def solution(mesh):
    return jax.shard_map(
        per_device,
        mesh=mesh,
        in_specs=(
            P(None, None, "lat", "lon"),
            P(),
            P(),
            P(),
            P(),
            P("lat", "lon", None, None),
            P("lat", "lon", None),
            P("lat", "lon", None, None),
            P("lat", "lon", None),
            P("lat", "lon", None, None),
            P("lat", "lon", None),
            P("lat", "lon", None),
        ),
        out_specs=(P(None, None, "lat", "lon"), P(None, "lat", "lon"), P("lat", "lon", None)),
        check_vma=False,
    )
```

time: 639 us -> 217 us (0.34); the launches traced: 630 us -> 216 us
  other arithmetic: 234 us -> 15.8 us
  local copies, waits for them, and re-layouts: 153 us -> 14.9 us
  matrix products: 62.8 us -> 5.07 us
  Pallas kernels: 0 us -> 55.6 us
  waiting for transfers between devices: 123 us -> 82.9 us
  blocking collectives: 12.7 us -> 0 us
    scatter-add x4 -> x0, other arithmetic: 176 us -> none  [the longest x2 88.9 us: per_device(): forcing = jnp.zeros((level_count, lat_rows * lon_cells), jnp.float32).at[...]
    ppermute x16 -> x10, waiting for transfers between devices: 88.8 us -> 10.4 us  [shift(): lax.ppermute(block, axis, [(i, (i + step) % count) for i in range(count)])]
    gather x4 -> x0, local copies, waits for them, and re-layouts: 76.1 us -> none  [the longest x2 45.6 us: per_device(): picked = jnp.take(observe_incoming.reshape(-1), gather_index)]
    dot_general x6 -> x3, matrix products: 62.8 us -> 5.07 us  [the longest x1 3.1 us: per_device(): lax.dot_general(sides3, place, (((1,), (0,)), ((), ())), preferred_elemen...]
    pallas_call x0 -> x7, Pallas kernels: none -> 55.6 us  [the longest x1 18 us: per_device(): pl.pallas_call(functools.partial(adjoint_kernel, scale), grid=(members //...]
    all_to_all x3 -> x7, waiting for transfers between devices: 34.7 us -> 72.5 us  [the longest x1 25.9 us: per_device(): lax.all_to_all(spread, both, split_axis=0, concat_axis=0, tiled=True)]
    mul x14 -> x2, other arithmetic: 36.5 us -> 0.07 us  [the longest x1 0.07 us: per_device(): lon_taps[None, :, None] * lon_taps[None, None, :]]
    ppermute x4 -> x0, local copies, waits for them, and re-layouts: 20.2 us -> none  [the longest x2 10.1 us: padded(): lax.ppermute(lax.slice_in_dim(block, block.shape[dim] - width, None, axis...]
  transfers between devices with their start and end apart: 19 -> 17, of which waited for: 11 -> 10; matrix products, arithmetic and copies ran while one was open for 21% -> 14% of each run, Pallas kernels for 0% -> 17%
where the time goes in v1:
time: 217 us; the launch traced here: 216 us
  waiting for transfers between devices  82.9 us (38%)
  Pallas kernels  55.6 us (26%)
  starting transfers between devices  39.5 us (18%)
  other arithmetic  15.8 us (7%)
  local copies, waits for them, and re-layouts  14.9 us (7%)
  matrix products  5.07 us (2%)
  between operations  2.25 us (1%)
    all_to_all x1, waiting for transfers between devices, per_device(): lax.all_to_all(spread, both, split_axis=0, concat_axis=0, tiled=True)  25.9 us
    all_to_all x5, waiting for transfers between devices, route(): return lax.all_to_all(buffer, both, split_axis=0, concat_axis=0, tiled=True)  24.4 us
    all_to_all x1, waiting for transfers between devices, per_device(): lax.all_to_all(send_count, both, split_axis=2, concat_axis=2, tiled=True)  22.2 us
    pallas_call x1, Pallas kernels, per_device(): pl.pallas_call(functools.partial(adjoint_kernel, scale), grid=(members //...  18 us
    all_to_all x5, starting transfers between devices, route(): return lax.all_to_all(buffer, both, split_axis=0, concat_axis=0, tiled=True)  17.1 us
    pallas_call x2, Pallas kernels, observe(): pl.pallas_call(functools.partial(obs_kernel, table is not None, chunk), o...  16.7 us
    ppermute x10, starting transfers between devices, shift(): lax.ppermute(block, axis, [(i, (i + step) % count) for i in range(count)])  13.6 us
    ppermute x10, waiting for transfers between devices, shift(): lax.ppermute(block, axis, [(i, (i + step) % count) for i in range(count)])  10.4 us
  transfers between devices with their start and end apart: 17, of which 10 were waited for; matrix products, arithmetic and copies ran while one was open for 14% of the time, Pallas kernels for 17%

profile of v1, /device:TPU:0, one launch (start us, length us, event | category | flops | bytes accessed | tf_op | source)
XLA Modules:
  0.0 215.9 jit_solution(6285481647099436248)
XLA Ops:
  4.5 6.1 %all-to-all-start = ((s32[1,1,32]{1,0,2:T(1,128)}), s32[1,1,32]{1,0,2:T(1,128)S(1)}, u32[]{:S(2)}, u32[]{:S(2)}) async-start(s32[1,1,32]{1,0,2:T(1,128)} %copy.33), calls=%async_computation | async-start | bytes 32768 | tf_op jit(solution)/shard_map/all_to_all | solution.py:269
  12.5 22.2 %all-to-all-done = s32[1,1,32]{1,0,2:T(1,128)S(1)} async-done(((s32[1,1,32]{1,0,2:T(1,128)}), s32[1,1,32]{1,0,2:T(1,128)S(1)}, u32[]{:S(2)}, u32[]{:S(2)}) %all-to-all-start) | async-done | bytes 160 | tf_op jit(solution)/shard_map/all_to_all | solution.py:269
  36.5 5.4 %observe.2 = (f32[1,2048]{1,0:T(1,128)}, f32[256,256]{1,0:T(8,128)}) custom-call(s32[4,2048]{1,0:T(4,128)} %get-tuple-element.25.refs_0_.refs_1_, s32[4,2048]{1,0:T(4,128)} %get-tuple-element.26.refs_1_.refs_2_, f32[4,2048]{1,0:T(4,128)} %bitcast.78, f32[1,2048]{1,0:T(1,128)} %bitcast.85, f32[1,2048]{1,0:T(1,128)} %bitcast.87), custom_call_target="tpu_custom_call" | custom-call | tf_op jit(solution)/shard_map/observe/pallas_call | solution.py:87
  41.9 5.0 %all-to-all-start.1 = ((f32[32,8,256]{2,1,0:T(8,128)}), f32[32,8,256]{2,1,0:T(8,128)S(1)}, u32[]{:S(2)}, u32[]{:S(2)}) async-start(f32[32,8,256]{2,1,0:T(8,128)} %bitcast.74), calls=%async_computation.1 | async-start | bytes 524288 | tf_op jit(solution)/shard_map/all_to_all | solution.py:368
  47.5 4.6 %collective-permute-start.3 = (bf16[8,5120]{1,0:T(8,128)(2,1)}, bf16[8,5120]{1,0:T(8,128)(2,1)}, u32[]{:S(2)}, u32[]{:S(2)}) collective-permute-start(bf16[8,5120]{1,0:T(8,128)(2,1)} %get-tuple-element.15), channel_id=1, source_target_pairs={{0,7},{1,0},{2,1},{3,2},{4,3},{5,4},{6,5},{7,6},{8,15},{9,8},{10,9... | collective-permute-start | bytes 245768 | tf_op jit(solution)/shard_map/ppermute | solution.py:224
  52.7 4.6 %all-to-all-done.1.values = f32[32,8,256]{2,1,0:T(8,128)S(1)} async-done(((f32[32,8,256]{2,1,0:T(8,128)}), f32[32,8,256]{2,1,0:T(8,128)S(1)}, u32[]{:S(2)}, u32[]{:S(2)}) %all-to-all-start.1) | async-done | bytes 262176 | tf_op jit(solution)/shard_map/all_to_all | solution.py:368
  58.0 4.8 %to_columns.2 = f32[64,128]{1,0:T(8,128)} custom-call(s32[32,256]{1,0:T(8,128)} %bitcast.70, f32[32,8,256]{2,1,0:T(8,128)} %copy-done.3), custom_call_target="tpu_custom_call" | custom-call | tf_op jit(solution)/shard_map/to_columns/pallas_call | solution.py:410
  65.5 4.2 %all-to-all-start.3 = ((f32[32,8,128]{2,1,0:T(8,128)}), f32[32,8,128]{2,1,0:T(8,128)S(1)}, u32[]{:S(2)}, u32[]{:S(2)}) async-start(f32[32,8,128]{2,1,0:T(8,128)} %bitcast.26), calls=%async_computation.3 | async-start | bytes 262144 | tf_op jit(solution)/shard_map/all_to_all | solution.py:368
  74.0 3.5 %all-to-all-done.3.forcing = f32[32,8,128]{2,1,0:T(8,128)S(1)} async-done(((f32[32,8,128]{2,1,0:T(8,128)}), f32[32,8,128]{2,1,0:T(8,128)S(1)}, u32[]{:S(2)}, u32[]{:S(2)}) %all-to-all-start.3) | async-done | bytes 131104 | tf_op jit(solution)/shard_map/all_to_all | solution.py:368
  78.2 2.7 %all-to-all-start.2 = ((bf16[32,20,8,128]{3,2,1,0:T(8,128)(2,1)}), bf16[32,20,8,128]{3,2,1,0:T(8,128)(2,1)S(1)}, u32[]{:S(2)}, u32[]{:S(2)}) async-start(bf16[32,20,8,128]{3,2,1,0:T(8,128)(2,1)} %bitcast.25), calls=%async_computation.2 | async-start | bytes 2621440 | tf_op jit(solution)/shard_map/all_to_all | solution.py:290
  88.1 25.9 %all-to-all-done.2.members = bf16[32,20,8,128]{3,2,1,0:T(8,128)(2,1)S(1)} async-done(((bf16[32,20,8,128]{3,2,1,0:T(8,128)(2,1)}), bf16[32,20,8,128]{3,2,1,0:T(8,128)(2,1)S(1)}, u32[]{:S(2)}, u32[]{:S(2)}) %all-to-all-start.2) | async-done | bytes 1310752 | tf_op jit(solution)/shard_map/all_to_all | solution.py:290
  115.1 6.7 %covariance.1 = f32[32,8,128]{2,1,0:T(8,128)} custom-call(f32[2]{0:T(128)} %pad_maximum_fusion.2.coef, bf16[32,20,8,128]{3,2,1,0:T(8,128)(2,1)} %copy-done.1, f32[32,8,128]{2,1,0:T(8,128)} %copy-done.5, f32[224,224]{1,0:T(8,128)} %fusion.8.lat_op, f32[384,128]{1,0:T(8,128)} %select_reduce_fusion.lon_op), custom_call_target="tpu_custom_call" | custom-call | tf_op jit(solution)/shard_map/covariance/pallas_call | solution.py:384
  125.2 6.9 %all-to-all-done.4 = f32[32,8,128]{2,1,0:T(8,128)S(1)} async-done(((f32[32,8,128]{2,1,0:T(8,128)}), f32[32,8,128]{2,1,0:T(8,128)S(1)}, u32[]{:S(2)}, u32[]{:S(2)}) %all-to-all-start.4) | async-done | bytes 131104 | tf_op jit(solution)/shard_map/all_to_all | solution.py:368
  132.8 4.4 %to_slots.1 = f32[32,8,256]{2,1,0:T(8,128)} custom-call(s32[32,256]{1,0:T(8,128)} %bitcast.71, f32[64,128]{1,0:T(8,128)} %bitcast.82), custom_call_target="tpu_custom_call" | custom-call | tf_op jit(solution)/shard_map/to_slots/pallas_call | solution.py:398
  137.3 2.8 %all-to-all-start.5 = ((f32[32,8,256]{2,1,0:T(8,128)}), f32[32,8,256]{2,1,0:T(8,128)S(1)}, u32[]{:S(2)}, u32[]{:S(2)}) async-start(f32[32,8,256]{2,1,0:T(8,128)} %to_slots.1), calls=%async_computation.5 | async-start | bytes 524288 | tf_op jit(solution)/shard_map/all_to_all | solution.py:368
  140.9 9.4 %all-to-all-done.5 = f32[32,8,256]{2,1,0:T(8,128)S(1)} async-done(((f32[32,8,256]{2,1,0:T(8,128)}), f32[32,8,256]{2,1,0:T(8,128)S(1)}, u32[]{:S(2)}, u32[]{:S(2)}) %all-to-all-start.5) | async-done | bytes 262176 | tf_op jit(solution)/shard_map/all_to_all | solution.py:368
  151.0 11.3 %observe.3 = (f32[1,2048]{1,0:T(1,128)}, f32[256,256]{1,0:T(8,128)}) custom-call(f32[256,256]{1,0:T(8,128)} %bitcast.67, s32[4,2048]{1,0:T(4,128)} %get-tuple-element.25.refs_0_.refs_1_, s32[4,2048]{1,0:T(4,128)} %get-tuple-element.26.refs_1_.refs_2_, f32[4,2048]{1,0:T(4,128)} %bitcast.79, f32[1,2048]{1,0:T(1,128)} %bitcast.86, f32[1,2048]{1,0:T(1,128)} %bitcast.88), custom_call_target="tpu_custom_call" | custom-call | tf_op jit(solution)/shard_map/observe/pallas_call | solution.py:87
  162.3 2.6 %all-to-all-start.6 = ((f32[32,8,256]{2,1,0:T(8,128)}), f32[32,8,256]{2,1,0:T(8,128)S(1)}, u32[]{:S(2)}, u32[]{:S(2)}) async-start(f32[32,8,256]{2,1,0:T(8,128)} %bitcast.73), calls=%async_computation.6 | async-start | bytes 524288 | tf_op jit(solution)/shard_map/all_to_all | solution.py:368
  167.2 5.6 %collective-permute-done.5 = bf16[16,5120]{1,0:T(8,128)(2,1)S(1)} collective-permute-done((bf16[16,5120]{1,0:T(8,128)(2,1)S(1)}, bf16[16,5120]{1,0:T(8,128)(2,1)S(1)}, u32[]{:S(2)}, u32[]{:S(2)}) %collective-permute-start.5) | collective-permute-done | bytes 163872 | tf_op jit(solution)/shard_map/ppermute | solution.py:224
  174.1 3.1 %fusion.2 = bf16[3,5120,128]{2,1,0:T(8,128)(2,1)} fusion(bf16[1,16,5120]{2,1,0:T(8,128)(2,1)S(1)} %bitcast.75, bf16[1,16,5120]{2,1,0:T(8,128)(2,1)S(1)} %bitcast.69, bf16[1,16,5120]{2,1,0:T(8,128)(2,1)S(1)} %bitcast.76), kind=kOutput, calls=%fused_computation.9 | convolution fusion | flops 63408128 | bytes 4423680 | tf_op jit(solution)/shard_map/dot_general | solution.py:309
  177.9 4.8 %to_columns.3 = f32[64,128]{1,0:T(8,128)} custom-call(s32[32,256]{1,0:T(8,128)} %bitcast.72, f32[32,8,256]{2,1,0:T(8,128)} %copy-done.2), custom_call_target="tpu_custom_call" | custom-call | tf_op jit(solution)/shard_map/to_columns/pallas_call | solution.py:410
  185.8 3.1 %collective-permute-start.7 = (f32[8,8,8]{2,1,0:T(8,128)S(1)}, f32[8,8,8]{2,1,0:T(8,128)S(1)}, u32[]{:S(2)}, u32[]{:S(2)}) collective-permute-start(f32[8,8,8]{2,1,0:T(8,128)S(1)} %get-tuple-element.20), channel_id=1, source_target_pairs={{0,7},{1,0},{2,1},{3,2},{4,3},{5,4},{6,5},{7,6},{8,15},{9,8},{10,9... | collective-permute-start | bytes 6152 | tf_op jit(solution)/shard_map/ppermute | solution.py:224
  188.9 3.4 %pad_maximum_fusion.members = bf16[3,80,8,8,128]{4,3,2,1,0:T(8,128)(2,1)} fusion(bf16[1,80,8,8,128]{4,3,2,1,0:T(8,128)(2,1)} %bitcast.2, bf16[1,80,8,8,128]{4,3,2,1,0:T(8,128)(2,1)S(1)} %bitcast.66, bf16[1,80,8,8,128]{4,3,2,1,0:T(8,128)(2,1)} %bitcast), kind=kLoop, calls=%fused_computation.2 | loop fusion | flops 3932160 | bytes 7864320 | tf_op jit(solution)/shard_map/stack | solution.py:306
  197.9 18.0 %adjoint.1 = (f32[80,8,8,128]{3,2,1,0:T(8,128)}, f32[8,8,128]{2,1,0:T(8,128)}) custom-call(bf16[3,80,8,8,128]{4,3,2,1,0:T(8,128)(2,1)} %pad_maximum_fusion.members, bf16[3,80,8,8,128]{4,3,2,1,0:T(8,128)(2,1)} %bitcast.63, f32[3,8,8,256]{3,2,1,0:T(8,128)} %pad_maximum_fusion.1.field, f32[8,8,128]{2,1,0:T(8,128)} %broadcast_in_dim.133.sigma, ...), custom_call_target="tpu_custom_call" | custom-call | tf_op jit(solution)/shard_map/adjoint/pallas_call | solution.py:433
  (107 shorter events, 42.6 us)
Async XLA Ops:
  0.6 34.8 %copy-start.8 = (s32[1,1,4,2048]{3,2,1,0:T(4,128)S(1)}, s32[1,1,4,2048]{3,2,1,0:T(4,128)}, u32[]{:S(2)}) copy-start(s32[1,1,4,2048]{3,2,1,0:T(4,128)} %param.19) | copy-start | bytes 98308
  0.6 35.2 %copy-start.9 = (s32[1,1,2048]{2,1,0:T(1,128)S(1)}, s32[1,1,2048]{2,1,0:T(1,128)}, u32[]{:S(2)}) copy-start(s32[1,1,2048]{2,1,0:T(1,128)} %param.20) | copy-start | bytes 24580
  0.7 188.3 %collective-permute-start.1 = (bf16[80,8,8,128]{3,2,1,0:T(8,128)(2,1)}, bf16[80,8,8,128]{3,2,1,0:T(8,128)(2,1)}, u32[]{:S(2)}, u32[]{:S(2)}) collective-permute-start(bf16[80,8,8,128]{3,2,1,0:T(8,128)(2,1)} %param.12), channel_id=1, source_target_pairs={{0,24},{8,0},{16,8},{24,16},{1,25},{9,1},{17,9},{25,17},{2,26},{10... | collective-permute-start | bytes 3932168 | tf_op jit(solution)/shard_map/ppermute | solution.py:224
  3.1 185.8 %collective-permute-start = (bf16[80,8,8,128]{3,2,1,0:T(8,128)(2,1)}, bf16[80,8,8,128]{3,2,1,0:T(8,128)(2,1)}, u32[]{:S(2)}, u32[]{:S(2)}) collective-permute-start(bf16[80,8,8,128]{3,2,1,0:T(8,128)(2,1)} %param.12), channel_id=1, source_target_pairs={{0,8},{8,16},{16,24},{24,0},{1,9},{9,17},{17,25},{25,1},{2,10},{10... | collective-permute-start | bytes 3932168 | tf_op jit(solution)/shard_map/ppermute | solution.py:224
  4.5 30.2 %all-to-all-start = ((s32[1,1,32]{1,0,2:T(1,128)}), s32[1,1,32]{1,0,2:T(1,128)S(1)}, u32[]{:S(2)}, u32[]{:S(2)}) async-start(s32[1,1,32]{1,0,2:T(1,128)} %copy.33), calls=%async_computation | async-start | bytes 32768 | tf_op jit(solution)/shard_map/all_to_all | solution.py:269
  10.6 41.4 %copy-start.10 = (f32[2]{0:T(128)S(1)}, f32[2]{0:T(128)}, u32[]{:S(2)}) copy-start(f32[2]{0:T(128)} %param.16) | copy-start | bytes 28
  12.4 57.4 %copy-start.13 = (f32[8]{0:T(128)S(1)}, f32[8]{0:T(128)}, u32[]{:S(2)}) copy-start(f32[8]{0:T(128)} %param.13) | copy-start | bytes 100
  12.4 59.2 %copy-start.12 = (f32[17]{0:T(128)S(1)}, f32[17]{0:T(128)}, u32[]{:S(2)}) copy-start(f32[17]{0:T(128)} %param.14) | copy-start | bytes 208
  12.4 59.3 %copy-start.11 = (f32[17]{0:T(128)S(1)}, f32[17]{0:T(128)}, u32[]{:S(2)}) copy-start(f32[17]{0:T(128)} %param.15) | copy-start | bytes 208
  36.5 36.3 %copy-start = (bf16[80,8,8,128]{3,2,1,0:T(8,128)(2,1)S(1)}, bf16[80,8,8,128]{3,2,1,0:T(8,128)(2,1)}, u32[]{:S(2)}) copy-start(bf16[80,8,8,128]{3,2,1,0:T(8,128)(2,1)} %param.12) | copy-start | bytes 3932164
  41.9 15.4 %all-to-all-start.1 = ((f32[32,8,256]{2,1,0:T(8,128)}), f32[32,8,256]{2,1,0:T(8,128)S(1)}, u32[]{:S(2)}, u32[]{:S(2)}) async-start(f32[32,8,256]{2,1,0:T(8,128)} %bitcast.74), calls=%async_computation.1 | async-start | bytes 524288 | tf_op jit(solution)/shard_map/all_to_all | solution.py:368
  47.5 117.4 %collective-permute-start.3 = (bf16[8,5120]{1,0:T(8,128)(2,1)}, bf16[8,5120]{1,0:T(8,128)(2,1)}, u32[]{:S(2)}, u32[]{:S(2)}) collective-permute-start(bf16[8,5120]{1,0:T(8,128)(2,1)} %get-tuple-element.15), channel_id=1, source_target_pairs={{0,7},{1,0},{2,1},{3,2},{4,3},{5,4},{6,5},{7,6},{8,15},{9,8},{10,9... | collective-permute-start | bytes 245768 | tf_op jit(solution)/shard_map/ppermute | solution.py:224
  52.1 88.0 %collective-permute-start.2 = (bf16[8,5120]{1,0:T(8,128)(2,1)}, bf16[8,5120]{1,0:T(8,128)(2,1)}, u32[]{:S(2)}, u32[]{:S(2)}) collective-permute-start(bf16[8,5120]{1,0:T(8,128)(2,1)} %get-tuple-element.16), channel_id=1, source_target_pairs={{0,1},{1,2},{2,3},{3,4},{4,5},{5,6},{6,7},{7,0},{8,9},{9,10},{10,1... | collective-permute-start | bytes 245768 | tf_op jit(solution)/shard_map/ppermute | solution.py:224
  65.5 12.0 %all-to-all-start.3 = ((f32[32,8,128]{2,1,0:T(8,128)}), f32[32,8,128]{2,1,0:T(8,128)S(1)}, u32[]{:S(2)}, u32[]{:S(2)}) async-start(f32[32,8,128]{2,1,0:T(8,128)} %bitcast.26), calls=%async_computation.3 | async-start | bytes 262144 | tf_op jit(solution)/shard_map/all_to_all | solution.py:368
  78.2 35.8 %all-to-all-start.2 = ((bf16[32,20,8,128]{3,2,1,0:T(8,128)(2,1)}), bf16[32,20,8,128]{3,2,1,0:T(8,128)(2,1)S(1)}, u32[]{:S(2)}, u32[]{:S(2)}) async-start(bf16[32,20,8,128]{3,2,1,0:T(8,128)(2,1)} %bitcast.25), calls=%async_computation.2 | async-start | bytes 2621440 | tf_op jit(solution)/shard_map/all_to_all | solution.py:290
  121.8 10.4 %all-to-all-start.4 = ((f32[32,8,128]{2,1,0:T(8,128)}), f32[32,8,128]{2,1,0:T(8,128)S(1)}, u32[]{:S(2)}, u32[]{:S(2)}) async-start(f32[32,8,128]{2,1,0:T(8,128)} %covariance.1), calls=%async_computation.4 | async-start | bytes 262144 | tf_op jit(solution)/shard_map/all_to_all | solution.py:368
  137.3 13.0 %all-to-all-start.5 = ((f32[32,8,256]{2,1,0:T(8,128)}), f32[32,8,256]{2,1,0:T(8,128)S(1)}, u32[]{:S(2)}, u32[]{:S(2)}) async-start(f32[32,8,256]{2,1,0:T(8,128)} %to_slots.1), calls=%async_computation.5 | async-start | bytes 524288 | tf_op jit(solution)/shard_map/all_to_all | solution.py:368
  162.3 14.8 %all-to-all-start.6 = ((f32[32,8,256]{2,1,0:T(8,128)}), f32[32,8,256]{2,1,0:T(8,128)S(1)}, u32[]{:S(2)}, u32[]{:S(2)}) async-start(f32[32,8,256]{2,1,0:T(8,128)} %bitcast.73), calls=%async_computation.6 | async-start | bytes 524288 | tf_op jit(solution)/shard_map/all_to_all | solution.py:368
  165.8 7.0 %collective-permute-start.5 = (bf16[16,5120]{1,0:T(8,128)(2,1)S(1)}, bf16[16,5120]{1,0:T(8,128)(2,1)S(1)}, u32[]{:S(2)}, u32[]{:S(2)}) collective-permute-start(bf16[16,5120]{1,0:T(8,128)(2,1)S(1)} %constant_dynamic-update-slice_fusion), channel_id=1, source_target_pairs={{0,24},{8,0},{16,8},{24,16},{1,25},{9,1},{17,9},{25,17},{2,26},{10... | collective-permute-start | bytes 491528 | tf_op jit(solution)/shard_map/ppermute | solution.py:224
  167.2 6.9 %collective-permute-start.4 = (bf16[16,5120]{1,0:T(8,128)(2,1)S(1)}, bf16[16,5120]{1,0:T(8,128)(2,1)S(1)}, u32[]{:S(2)}, u32[]{:S(2)}) collective-permute-start(bf16[16,5120]{1,0:T(8,128)(2,1)S(1)} %constant_dynamic-update-slice_fusion), channel_id=1, source_target_pairs={{0,8},{8,16},{16,24},{24,0},{1,9},{9,17},{17,25},{25,1},{2,10},{10... | collective-permute-start | bytes 491528 | tf_op jit(solution)/shard_map/ppermute | solution.py:224
  184.2 8.1 %collective-permute-start.6 = (f32[8,8,8]{2,1,0:T(8,128)S(1)}, f32[8,8,8]{2,1,0:T(8,128)S(1)}, u32[]{:S(2)}, u32[]{:S(2)}) collective-permute-start(f32[8,8,8]{2,1,0:T(8,128)S(1)} %get-tuple-element.19), channel_id=1, source_target_pairs={{0,1},{1,2},{2,3},{3,4},{4,5},{5,6},{6,7},{7,0},{8,9},{9,10},{10,1... | collective-permute-start | bytes 6152 | tf_op jit(solution)/shard_map/ppermute | solution.py:224
  185.8 6.5 %collective-permute-start.7 = (f32[8,8,8]{2,1,0:T(8,128)S(1)}, f32[8,8,8]{2,1,0:T(8,128)S(1)}, u32[]{:S(2)}, u32[]{:S(2)}) collective-permute-start(f32[8,8,8]{2,1,0:T(8,128)S(1)} %get-tuple-element.20), channel_id=1, source_target_pairs={{0,7},{1,0},{2,1},{3,2},{4,3},{5,4},{6,5},{7,6},{8,15},{9,8},{10,9... | collective-permute-start | bytes 6152 | tf_op jit(solution)/shard_map/ppermute | solution.py:224
  192.4 2.6 %collective-permute-start.9 = (f32[8,8,256]{2,1,0:T(8,128)S(1)}, f32[8,8,256]{2,1,0:T(8,128)S(1)}, u32[]{:S(2)}, u32[]{:S(2)}) collective-permute-start(f32[8,8,256]{2,1,0:T(8,128)S(1)} %maximum_maximum_fusion.1), channel_id=1, source_target_pairs={{0,24},{8,0},{16,8},{24,16},{1,25},{9,1},{17,9},{25,17},{2,26},{10... | collective-permute-start | bytes 196616 | tf_op jit(solution)/shard_map/ppermute | solution.py:224
  192.8 3.7 %collective-permute-start.8 = (f32[8,8,256]{2,1,0:T(8,128)S(1)}, f32[8,8,256]{2,1,0:T(8,128)S(1)}, u32[]{:S(2)}, u32[]{:S(2)}) collective-permute-start(f32[8,8,256]{2,1,0:T(8,128)S(1)} %maximum_maximum_fusion.1), channel_id=1, source_target_pairs={{0,8},{8,16},{16,24},{24,0},{1,9},{9,17},{17,25},{25,1},{2,10},{10... | collective-permute-start | bytes 196616 | tf_op jit(solution)/shard_map/ppermute | solution.py:224
  (7 other events, 13.1 us)

commit v2 on v1

v2 whole, which is shorter than its diff:
```python
import functools
import math

import jax
import jax.numpy as jnp
from jax import lax
from jax.experimental import pallas as pl
from jax.experimental.pallas import tpu as pltpu
from jax.sharding import PartitionSpec as P

HYBRID_STATIC = 0.5
HYBRID_ENSEMBLE = 0.8660254037844386
BF16 = jnp.bfloat16
F32 = jnp.float32
MESH = pl.DeviceIdType.MESH
VMEM = pl.BlockSpec(memory_space=pltpu.VMEM)


def halves(x):
    high = x.astype(BF16)
    return high, (x - high.astype(F32)).astype(BF16)


def dot(a, b):
    return jnp.dot(a, b, preferred_element_type=F32)


def dot_nt(a, b):
    return lax.dot_general(a, b, (((1,), (1,)), ((), ())), preferred_element_type=F32)


def dot3(a, b):
    a_high, a_low = halves(a)
    b_high, b_low = halves(b)
    return dot(a_high, b_high) + dot(a_high, b_low) + dot(a_low, b_high)


def iota(shape, dim):
    return lax.broadcasted_iota(jnp.int32, shape, dim)


def obs_step(table, hi, lo, weight, innov, prec, departure, out, rows, slots):
    chunk = 512 if rows <= 256 else 256
    points = hi.shape[0]
    if table is not None:
        table_high, table_low = halves(table[...].reshape(rows, slots))

    def step(index, carry):
        where = pl.ds(pl.multiple_of(index * chunk, chunk), chunk)
        row_ids = iota((rows, chunk), 0)
        slot_ids = iota((slots, chunk), 0)
        value = -innov[:, where]
        if table is not None:
            for q in range(points):
                lo_hot = jnp.where(slot_ids == lo[q : q + 1, where], 1.0, 0.0).astype(BF16)
                product = dot(table_high, lo_hot) + dot(table_low, lo_hot)
                picked = jnp.sum(
                    jnp.where(row_ids == hi[q : q + 1, where], product, 0.0), axis=0, keepdims=True
                )
                value = value + weight[q : q + 1, where] * picked
            departure[:, where] = value
        value = prec[:, where] * value
        total = None
        for q in range(points):
            lo_hot = jnp.where(slot_ids == lo[q : q + 1, where], 1.0, 0.0).astype(BF16)
            pushed = weight[q : q + 1, where] * value
            high = pushed.astype(BF16).astype(F32)
            chosen = row_ids == hi[q : q + 1, where]
            term = dot_nt(jnp.where(chosen, high, 0.0).astype(BF16), lo_hot) + dot_nt(
                jnp.where(chosen, pushed - high, 0.0).astype(BF16), lo_hot
            )
            total = term if total is None else total + term
        return carry + total

    total = lax.fori_loop(0, hi.shape[1] // chunk, step, jnp.zeros((rows, slots), F32))
    out[...] = total.reshape(out.shape)


def to_slots(cols, field, out):
    levels, lat_rows, cells = field.shape
    slots = out.shape[2]
    width = cols.shape[1]
    per_row = width // slots
    rows = jnp.concatenate([field[:, r, :] for r in range(lat_rows)], axis=0)
    count = rows.shape[0]
    both = jnp.concatenate(halves(rows), axis=0)

    def step(index, carry):
        col = cols[pl.ds(index, 1), :]
        cell_hot = jnp.where(iota((cells, width), 0) == col % cells, 1.0, 0.0).astype(BF16)
        product = dot(both, cell_hot)
        product = product[:count] + product[count:]
        row = jnp.broadcast_to(col // cells, (levels, width))
        total = jnp.zeros((levels, width), F32)
        for r in range(lat_rows):
            total = jnp.where(row == r, product[r * levels : (r + 1) * levels], total)
        for j in range(per_row):
            out[index * per_row + j] = total[:, j * slots : (j + 1) * slots]
        return carry

    lax.fori_loop(0, cols.shape[0], step, 0)


def to_columns(cols, values, shape):
    levels, lat_rows, cells = shape
    slots = values.shape[2]
    width = cols.shape[1]
    per_row = width // slots
    count = levels * lat_rows

    def step(index, total):
        col = cols[pl.ds(index, 1), :]
        cell_hot = jnp.where(iota((cells, width), 0) == col % cells, 1.0, 0.0).astype(BF16)
        chosen = iota((lat_rows, width), 0) == col // cells
        value = values[index * per_row]
        if per_row > 1:
            value = jnp.concatenate(
                [values[index * per_row + j] for j in range(per_row)], axis=1
            )
        high = value.astype(BF16).astype(F32)
        low = value - high
        parts = [jnp.where(chosen, high[l : l + 1], 0.0) for l in range(levels)]
        parts += [jnp.where(chosen, low[l : l + 1], 0.0) for l in range(levels)]
        return total + dot_nt(jnp.concatenate(parts, axis=0).astype(BF16), cell_hot)

    total = lax.fori_loop(0, cols.shape[0], step, jnp.zeros((2 * count, cells), F32))
    return (total[:count] + total[count:]).reshape(shape)


def covariance(blocks_lat, blocks_lon, coef, members, forcing, lat_op, lon_op, out, wide, mid):
    count = members.shape[1]
    rows, cells = forcing.shape[1:]
    height = blocks_lat * rows
    fields = count + 1
    for b in range(blocks_lon):
        for a in range(blocks_lat):
            spot = a * blocks_lon + b
            part = forcing[spot]
            for k in range(fields):
                piece = part if k == count else members[spot, k].astype(F32) * part
                at = pl.ds(k * height + a * rows, rows)
                wide[at, (b + 1) * cells : (b + 2) * cells] = piece
                if b == 0:
                    wide[at, (blocks_lon + 1) * cells :] = piece
                if b == blocks_lon - 1:
                    wide[at, :cells] = piece
    lon_high, lon_low = halves(lon_op[...])
    for b in range(blocks_lon):
        high, low = halves(wide[:, b * cells : (b + 3) * cells])
        mid[:, b * cells : (b + 1) * cells] = (
            dot(high, lon_high) + dot(high, lon_low) + dot(low, lon_high)
        )
    size = lat_op.shape[0]
    group = size // height
    for first in range(0, fields, group):
        where = pl.ds(first * height, size)
        wide[where, : blocks_lon * cells] = dot3(lat_op[...], mid[where, :])
    for a in range(blocks_lat):
        for b in range(blocks_lon):
            spot = a * blocks_lon + b
            total = coef[0] * wide[
                pl.ds(count * height + a * rows, rows), b * cells : (b + 1) * cells
            ]
            for k in range(count):
                total = total + coef[1] * (
                    members[spot, k].astype(F32)
                    * wide[pl.ds(k * height + a * rows, rows), b * cells : (b + 1) * cells]
                )
            out[spot] = total


def main_kernel(
    n_lat, n_lon, iterations,
    coef, step, ens, sides, count_row, cols, pos, level, weight, innov, prec, lat_op, lon_op,
    departure, near, near_sides, near_held,
    counts, whole, pushed, incoming, field, part, part_in, packed, table, held, wide, mid, hi, lo,
    ex_send, ex_recv, near_send, near_recv, side_send, side_recv, held_send, held_recv,
):
    lat_at, lon_at = lax.axis_index("lat"), lax.axis_index("lon")
    me = lat_at * n_lon + lon_at
    devices = n_lat * n_lon
    levels, rows, cells = held.shape
    slots = pushed.shape[2]
    per_group = whole.shape[1]
    half = sides.shape[0] // 2

    def place(d):
        return (d // n_lon, d % n_lon)

    barrier = pltpu.get_barrier_semaphore()

    def greet(k, carry):
        pl.semaphore_signal(
            barrier, inc=1, device_id=place((me + k) % devices), device_id_type=MESH
        )
        return carry

    lax.fori_loop(1, devices, greet, 0)
    pl.semaphore_wait(barrier, devices - 1)

    def send(source, target, number, first=1, last=None):
        def one(k, carry):
            d = (me + k) % devices
            pltpu.make_async_remote_copy(
                src_ref=source(d),
                dst_ref=target.at[me],
                send_sem=ex_send.at[number],
                recv_sem=ex_recv.at[number],
                device_id=place(d),
                device_id_type=MESH,
            ).start()
            return carry

        lax.fori_loop(first, devices if last is None else last, one, 0)

    def wait(target, number):
        every = target.at[pl.ds(0, devices - 1)]
        copy = pltpu.make_async_remote_copy(
            src_ref=every,
            dst_ref=every,
            send_sem=ex_send.at[number],
            recv_sem=ex_recv.at[number],
            device_id=place((me + 1) % devices),
            device_id_type=MESH,
        )
        copy.wait_send()
        copy.wait_recv()

    def members_of(d):
        return ens.at[pl.ds((d // levels) * per_group, per_group), d % levels]

    send(lambda d: count_row, counts, 0)
    early = max(2, devices // 4)
    send(members_of, whole, 1, 1, early)
    counts[me] = count_row[...]
    whole[me] = ens[pl.ds((me // levels) * per_group, per_group), me % levels]
    wait(counts, 0)
    received = jnp.concatenate([counts[d] for d in range(devices)], axis=0)
    width = received.shape[1]
    column = jnp.sum(
        jnp.where(iota((devices, width), 1) == me, received, 0), axis=1, keepdims=True
    )
    as_row = jnp.sum(
        jnp.where(iota((devices, width), 0) == iota((devices, width), 1), column, 0),
        axis=0, keepdims=True,
    )
    ends = jnp.sum(
        jnp.where(iota((devices, width), 1) <= iota((devices, width), 0), as_row, 0),
        axis=1, keepdims=True,
    )
    for q in range(pos.shape[0]):
        place_q = pos[q : q + 1, :]
        past = place_q >= ends
        source = jnp.sum(jnp.where(past, 1, 0), axis=0, keepdims=True)
        lo[q : q + 1, :] = place_q - jnp.sum(jnp.where(past, column, 0), axis=0, keepdims=True)
        hi[q : q + 1, :] = source * levels + level[...]

    number = 2
    for iteration in range(iterations):
        before = iteration - 1
        if iteration > 0:
            send(lambda d: held.at[d % levels], field.at[before], number)
            field[before, me] = held[me % levels]
            if iteration == 1:
                wait(whole, 1)
            wait(field.at[before], number)
            if iteration == 1:
                near_copies(
                    n_lat, n_lon, lat_at, lon_at, half, ens, sides, near, near_sides,
                    near_send, near_recv, side_send, side_recv, True,
                )
            covariance(
                n_lat, n_lon, coef, whole, field.at[before], lat_op, lon_op, part, wide, mid
            )
            send(lambda d: part.at[d], part_in.at[before], number + 1)
            part_in[before, me] = part[me]
            wait(part_in.at[before], number + 1)
            total = part_in[before, 0:levels]
            for g in range(1, devices // levels):
                total = total + part_in[before, g * levels : (g + 1) * levels]
            part[0:levels] = total
            to_slots(cols, part.at[0:levels], packed)
            send(lambda d: packed.at[d], table.at[before], number + 2)
            table[before, me] = packed[me]
            wait(table.at[before], number + 2)
            number += 3
        obs_step(
            table.at[before] if iteration > 0 else None,
            hi, lo, weight, innov, prec, departure, pushed, devices * levels, slots,
        )
        send(lambda d: pushed.at[d], incoming.at[iteration], number)
        if iteration == 0:
            send(members_of, whole, 1, early)
        incoming[iteration, me] = pushed[me]
        wait(incoming.at[iteration], number)
        number += 1
        forcing = to_columns(cols, incoming.at[iteration], held.shape)
        if iteration == 0:
            held[...] = -step[0] * forcing
        else:
            held[...] = held[...] - step[iteration] * (forcing + held[...])

    held_copies(n_lat, n_lon, lat_at, lon_at, held, near_held, held_send, held_recv, True)
    near_held[1, 1] = held[...]
    near_copies(
        n_lat, n_lon, lat_at, lon_at, half, ens, sides, near, near_sides,
        near_send, near_recv, side_send, side_recv, False,
    )
    held_copies(n_lat, n_lon, lat_at, lon_at, held, near_held, held_send, held_recv, False)


def exchange_pair(begin, has_send, has_recv, **copy):
    made = pltpu.make_async_remote_copy(device_id_type=MESH, **copy)
    if begin:
        pl.when(has_send)(made.start)
    else:
        pl.when(has_send)(made.wait_send)
        pl.when(has_recv)(made.wait_recv)


def lat_has(n_lat, lat_at, step):
    send = jnp.logical_and(lat_at + step >= 0, lat_at + step < n_lat)
    recv = jnp.logical_and(lat_at - step >= 0, lat_at - step < n_lat)
    return send, recv


def near_copies(
    n_lat, n_lon, lat_at, lon_at, half, ens, sides, near, near_sides,
    near_send, near_recv, side_send, side_recv, begin,
):
    for index, step in enumerate((1, -1)):
        has = lat_has(n_lat, lat_at, step)
        exchange_pair(
            begin, *has,
            src_ref=ens, dst_ref=near.at[index],
            send_sem=near_send.at[index], recv_sem=near_recv.at[index],
            device_id=((lat_at + step + n_lat) % n_lat, lon_at),
        )
    for up, step in enumerate((1, 0, -1)):
        has = lat_has(n_lat, lat_at, step)
        for side, turn in enumerate((1, -1)):
            exchange_pair(
                begin, *has,
                src_ref=sides.at[pl.ds(side * half, half)],
                dst_ref=near_sides.at[up, pl.ds(side * half, half)],
                send_sem=side_send.at[up * 2 + side], recv_sem=side_recv.at[up * 2 + side],
                device_id=((lat_at + step + n_lat) % n_lat, (lon_at + turn + n_lon) % n_lon),
            )


def held_copies(n_lat, n_lon, lat_at, lon_at, held, near_held, held_send, held_recv, begin):
    for up, step in enumerate((1, 0, -1)):
        has = lat_has(n_lat, lat_at, step)
        for side, turn in enumerate((1, 0, -1)):
            if step == 0 and turn == 0:
                continue
            exchange_pair(
                begin, *has,
                src_ref=held, dst_ref=near_held.at[up, side],
                send_sem=held_send.at[up * 3 + side], recv_sem=held_recv.at[up * 3 + side],
                device_id=((lat_at + step + n_lat) % n_lat, (lon_at + turn + n_lon) % n_lon),
            )


def adjoint_kernel(scale, keep, members, near, edges, field, sigma, lon_op, lat_op, out, static_out):
    batch, levels, rows, cells = out.shape
    lon_high, lon_low = halves(lon_op[...])

    def smooth(pieces, count):
        passes = []
        for piece in pieces:
            high, low = halves(piece)
            passes.append(
                (dot(high, lon_high) + dot(high, lon_low) + dot(low, lon_high)).reshape(
                    count, rows, cells
                )
            )
        stacked = jnp.concatenate(passes, axis=1)
        group = lat_op.shape[0] // rows
        results = []
        for first in range(0, count, group):
            results.append(
                dot3(
                    lat_op[...],
                    stacked[first : first + group].reshape(group * 3 * rows, cells),
                )
            )
        return jnp.concatenate(results, axis=0)

    count = batch * levels
    pieces = []
    for part in range(3):
        values = members[...] if part == 1 else near[part // 2]
        block = values.astype(F32) * field[part, :, :, :cells][None]
        edge = edges[part].astype(F32) * field[part, :, :, cells:][None]
        piece = jnp.concatenate([block, edge], axis=-1).reshape(count * rows, 2 * cells)
        pieces.append(piece if part == 1 else jnp.where(keep[part // 2] > 0, piece, 0.0))
    out[...] = scale * smooth(pieces, count).reshape(out.shape)

    @pl.when(pl.program_id(0) == 0)
    def _():
        pieces = [field[part].reshape(levels * rows, 2 * cells) for part in range(3)]
        static_out[...] = sigma[...] * smooth(pieces, levels).reshape(static_out.shape)


def shift(block, axis, step):
    count = lax.axis_size(axis)
    return lax.ppermute(block, axis, [(i, (i + step) % count) for i in range(count)])


def toeplitz(taps, shape, centre):
    offset = iota(shape, 0) - iota(shape, 1) + centre
    return jnp.sum(
        jnp.where(offset[:, :, None] == iota((1, 1, taps.shape[0]), 2), taps[None, None, :], 0.0),
        axis=2,
    )


def block_diagonal(matrix, count):
    rows, cols = matrix.shape
    tiled = jnp.tile(matrix, (count, count))
    return jnp.where(iota(tiled.shape, 0) // rows == iota(tiled.shape, 1) // cols, tiled, 0.0)


def divisor(count, limit):
    return max(n for n in range(1, count + 1) if count % n == 0 and (n <= limit or n == 1))


def per_device(
    ensemble,
    static_sigma,
    lat_taps,
    lon_taps,
    step_len,
    send_cols,
    send_count,
    obs_ref,
    obs_level,
    obs_weight,
    innovation,
    obs_precision,
):
    members, levels, rows, cells = ensemble.shape
    half = (lat_taps.shape[0] - 1) // 2
    n_lat, n_lon = lax.axis_size("lat"), lax.axis_size("lon")
    devices = n_lat * n_lon
    slots = send_cols.shape[3]
    scale = HYBRID_ENSEMBLE / math.sqrt(members - 1)
    lat_at = lax.axis_index("lat")
    lon_at = lax.axis_index("lon")

    positions = obs_ref.reshape(obs_ref.shape[2], -1)
    weight = obs_weight.reshape(positions.shape)
    groups = devices // levels
    per_group = members // groups
    device_at = lat_at * n_lon + lon_at
    level_at = device_at % levels

    pick = jnp.concatenate(
        [
            (iota((half, cells), 1) == iota((half, cells), 0) + cells - half),
            (iota((half, cells), 1) == iota((half, cells), 0)),
        ],
        axis=0,
    ).astype(BF16)
    sides = lax.dot_general(
        pick,
        ensemble.reshape(-1, cells),
        (((1,), (1,)), ((), ())),
        preferred_element_type=BF16,
    )

    whole_lat = toeplitz(lat_taps, (n_lat * rows, n_lat * rows), half).T
    lat_cov = jnp.dot(whole_lat, whole_lat.T, precision=lax.Precision.HIGHEST)
    lat_cov = block_diagonal(
        lat_cov, divisor(per_group + 1, max(1, 256 // (n_lat * rows)))
    )
    lon_corr = jnp.sum(
        jnp.where(
            iota((4 * half + 1, lon_taps.shape[0], lon_taps.shape[0]), 1)
            - iota((4 * half + 1, lon_taps.shape[0], lon_taps.shape[0]), 2)
            + 2 * half
            == iota((4 * half + 1, lon_taps.shape[0], lon_taps.shape[0]), 0),
            lon_taps[None, :, None] * lon_taps[None, None, :],
            0.0,
        ),
        axis=(1, 2),
    )
    lon_cov = toeplitz(lon_corr, (3 * cells, cells), 2 * half - cells)
    reverse = lon_taps[::-1]
    extended = toeplitz(reverse, (cells + 2 * half, cells), 0)
    lon_adjoint = jnp.concatenate(
        [
            extended[half : half + cells],
            extended[:half],
            extended[half + cells :],
            jnp.zeros((cells - 2 * half, cells), F32),
        ],
        axis=0,
    )
    lat_adjoint = block_diagonal(
        toeplitz(lat_taps[::-1], (rows + 2 * half, rows), 0).T, levels
    )

    wide_slots = max(slots, 256)
    cols = send_cols.reshape(-1, wide_slots)
    iterations = step_len.shape[0]
    later = max(1, iterations - 1)
    fields = per_group + 1
    height = n_lat * rows
    static_coef = jnp.where(
        device_at < levels, HYBRID_STATIC**2 * static_sigma[level_at] ** 2, 0.0
    )
    coef = jnp.stack([static_coef, jnp.full((), scale * scale, F32)])
    count_width = -(-devices // 128) * 128
    count_row = jnp.pad(send_count.reshape(1, -1), ((0, 0), (0, count_width - devices)))
    smem = pl.BlockSpec(memory_space=pltpu.SMEM)
    hbm = pl.BlockSpec(memory_space=pl.ANY)
    exchanges = 2 + iterations + 3 * (iterations - 1)
    departure, near, near_sides, near_held = pl.pallas_call(
        functools.partial(main_kernel, n_lat, n_lon, iterations),
        out_shape=(
            jax.ShapeDtypeStruct((1, positions.shape[1]), F32),
            jax.ShapeDtypeStruct((2,) + ensemble.shape, BF16),
            jax.ShapeDtypeStruct((3,) + sides.shape, BF16),
            jax.ShapeDtypeStruct((3, 3, levels, rows, cells), F32),
        ),
        in_specs=[smem] * 2 + [VMEM] * 11,
        out_specs=(VMEM, hbm, VMEM, VMEM),
        scratch_shapes=[
            pltpu.VMEM((devices, 1, count_width), jnp.int32),
            pltpu.VMEM((devices, per_group, rows, cells), BF16),
            pltpu.VMEM((devices, levels, slots), F32),
            pltpu.VMEM((iterations, devices, levels, slots), F32),
            pltpu.VMEM((later, devices, rows, cells), F32),
            pltpu.VMEM((devices, rows, cells), F32),
            pltpu.VMEM((later, devices, rows, cells), F32),
            pltpu.VMEM((devices, levels, slots), F32),
            pltpu.VMEM((later, devices, levels, slots), F32),
            pltpu.VMEM((levels, rows, cells), F32),
            pltpu.VMEM((fields * height, (n_lon + 2) * cells), F32),
            pltpu.VMEM((fields * height, n_lon * cells), F32),
            pltpu.VMEM(positions.shape, jnp.int32),
            pltpu.VMEM(positions.shape, jnp.int32),
            pltpu.SemaphoreType.DMA((exchanges,)),
            pltpu.SemaphoreType.DMA((exchanges,)),
            pltpu.SemaphoreType.DMA((2,)),
            pltpu.SemaphoreType.DMA((2,)),
            pltpu.SemaphoreType.DMA((6,)),
            pltpu.SemaphoreType.DMA((6,)),
            pltpu.SemaphoreType.DMA((9,)),
            pltpu.SemaphoreType.DMA((9,)),
        ],
        compiler_params=pltpu.CompilerParams(collective_id=0, has_side_effects=True),
        name="analysis",
    )(
        coef, step_len, ensemble, sides, count_row, cols, positions,
        obs_level.reshape(1, -1), weight, innovation.reshape(1, -1),
        obs_precision.reshape(1, -1), lat_cov, lon_cov,
    )
    wide3 = jnp.concatenate(
        [
            near_held[:, 1],
            near_held[:, 0, :, :, cells - half :],
            near_held[:, 2, :, :, :half],
            jnp.zeros((3, levels, rows, cells - 2 * half), F32),
        ],
        axis=3,
    )
    keep = jnp.stack([lat_at > 0, lat_at < n_lat - 1]).astype(jnp.int32)
    wide3 = jnp.where(
        jnp.stack([keep[0], jnp.ones((), jnp.int32), keep[1]])[:, None, None, None] > 0, wide3, 0.0
    )
    sides_id = (iota((2 * half, cells), 0) == iota((2 * half, cells), 1)).astype(BF16)
    edges3 = lax.dot_general(
        near_sides, sides_id, (((1,), (0,)), ((), ())), preferred_element_type=BF16
    ).reshape((3,) + ensemble.shape)
    batch = divisor(members, 8)
    sigma = jnp.broadcast_to(
        (HYBRID_STATIC * static_sigma)[:, None, None], (levels, rows, cells)
    )
    own_spec = pl.BlockSpec((batch, levels, rows, cells), lambda k: (k, 0, 0, 0))
    near_spec = pl.BlockSpec((2, batch, levels, rows, cells), lambda k: (0, k, 0, 0, 0))
    edge_spec = pl.BlockSpec((3, batch, levels, rows, cells), lambda k: (0, k, 0, 0, 0))
    control, static = pl.pallas_call(
        functools.partial(adjoint_kernel, scale),
        grid=(members // batch,),
        out_shape=(
            jax.ShapeDtypeStruct(ensemble.shape, F32),
            jax.ShapeDtypeStruct((levels, rows, cells), F32),
        ),
        in_specs=[smem, own_spec, near_spec, edge_spec] + [VMEM] * 4,
        out_specs=(
            pl.BlockSpec((batch, levels, rows, cells), lambda k: (k, 0, 0, 0)),
            pl.BlockSpec((levels, rows, cells), lambda k: (0, 0, 0)),
        ),
        name="adjoint",
    )(keep, ensemble, near, edges3, wide3, sigma, lon_adjoint, lat_adjoint)
    return control, static, departure.reshape(1, 1, -1)


def solution(mesh):
    return jax.shard_map(
        per_device,
        mesh=mesh,
        in_specs=(
            P(None, None, "lat", "lon"),
            P(),
            P(),
            P(),
            P(),
            P("lat", "lon", None, None),
            P("lat", "lon", None),
            P("lat", "lon", None, None),
            P("lat", "lon", None),
            P("lat", "lon", None, None),
            P("lat", "lon", None),
            P("lat", "lon", None),
        ),
        out_specs=(P(None, None, "lat", "lon"), P(None, "lat", "lon"), P("lat", "lon", None)),
        check_vma=False,
    )
```

time: 217 us -> 159 us (0.73)
  waiting for transfers between devices: 82.9 us -> 0 us
  Pallas kernels: 55.6 us -> 132 us
  starting transfers between devices: 39.5 us -> 0 us
  local copies, waits for them, and re-layouts: 14.9 us -> 8.32 us
  other arithmetic: 15.8 us -> 9.4 us
    pallas_call x6 -> x1, Pallas kernels: 37.5 us -> 114 us  [per_device(): pl.pallas_call(functools.partial(main_kernel, n_lat, n_lon, iterations),...]
    all_to_all x7 -> x0, waiting for transfers between devices: 72.5 us -> none  [the longest x1 25.9 us: per_device(): lax.all_to_all(spread, both, split_axis=0, concat_axis=0, tiled=True)]
    all_to_all x7 -> x0, starting transfers between devices: 25.8 us -> none  [the longest x5 17.1 us: route(): return lax.all_to_all(buffer, both, split_axis=0, concat_axis=0, tiled=True)]
    ppermute x10 -> x0, starting transfers between devices: 13.6 us -> none  [shift(): lax.ppermute(block, axis, [(i, (i + step) % count) for i in range(count)])]
    ppermute x10 -> x0, waiting for transfers between devices: 10.4 us -> none  [shift(): lax.ppermute(block, axis, [(i, (i + step) % count) for i in range(count)])]
    unnamed x30 -> x5, local copies, waits for them, and re-layouts: 6.71 us -> 0.61 us
    another operation x7 -> x0, other arithmetic: 4.33 us -> none  [the longest x1 3.36 us: per_device(): jnp.stack([shift(ensemble, 'lat', 1), ensemble, shift(ensemble, 'lat', -1)])]
    sub x2 -> x0, other arithmetic: 2.81 us -> none  [per_device(): held = held - step_len[iteration] * (forcing + held)]
  transfers between devices with their start and end apart: 17 -> 0, of which waited for: 10 -> 0; matrix products, arithmetic and copies ran while one was open for 14% -> 0% of each run, Pallas kernels for 17% -> 0%
where the time goes in v2:
time: 159 us
  Pallas kernels  132 us (83%)
  other arithmetic  9.4 us (6%)
  local copies, waits for them, and re-layouts  8.32 us (5%)
  matrix products  6.79 us (4%)
  between operations  2.09 us (1%)
    pallas_call x1, Pallas kernels, per_device(): pl.pallas_call(functools.partial(main_kernel, n_lat, n_lon, iterations),...  114 us
    pallas_call x1, Pallas kernels, per_device(): pl.pallas_call(functools.partial(adjoint_kernel, scale), grid=(members //...  18.2 us
    dot_general x1, matrix products, per_device(): lax.dot_general(near_sides, sides_id, (((1,), (0,)), ((), ())), preferred...  4.15 us

profile of v2, /device:TPU:0, one launch (start us, length us, event | category | flops | bytes accessed | tf_op | source)
XLA Modules:
  0.0 158.9 jit_solution(1507036057296033316)
XLA Ops:
  0.7 1.2 dynamic_slice.3
  3.3 0.6 pad_maximum_fusion.coef
  3.9 1.2 pad.4.count_row
  5.1 0.7 broadcast_multiply_fusion.1
  5.7 0.7 rev.7
  6.5 0.7 rev.6
  7.4 0.7 fusion.11
  8.0 1.4 add_compare_fusion
  9.6 0.8 broadcast_multiply_fusion
  10.6 0.8 select_reduce_fusion.2
  11.5 0.7 broadcast_in_dim.113.sigma
  12.5 0.8 maximum_maximum_fusion.lon_op
  13.2 2.4 %fusion.5.sides = bf16[16,5120]{1,0:T(8,128)(2,1)} fusion(bf16[5120,128]{1,0:T(8,128)(2,1)} %bitcast.31, pred[8,128]{1,0:T(8,128)(4,1)S(1)} %get-tuple-element.21, pred[8,128]{1,0:T(8,128)(4,1)S(1)} %get-tuple-element.22), kind=kOutput, calls=%fused_computation.25 | convolution fusion | flops 20973568 | bytes 1476608 | tf_op jit(solution)/shard_map/dot_general | solution.py:466
  15.7 1.4 select_reduce_fusion.lon_op
  17.2 0.7 fusion.1.lat_op
  18.0 0.2 tile.9
  18.3 0.8 fusion.lat_op
  19.1 114.2 %analysis.1 = (f32[1,2048]{1,0:T(1,128)}, bf16[2,80,8,8,128]{4,3,2,1,0:T(8,128)(2,1)}, bf16[3,16,5120]{2,1,0:T(8,128)(2,1)}, f32[3,3,8,8,128]{4,3,2,1,0:T(8,128)}) custom-call(f32[2]{0:T(128)} %pad_maximum_fusion.coef, f32[2]{0:T(128)} %step.1, bf16[80,8,8,128]{3,2,1,0:T(8,128)(2,1)} %members.1, bf16[16,5120]{1,0:T(8,128)(2,1)} %fusion.5.sides, ...), custom_call_target="tpu_custom_call" | custom-call | tf_op jit(solution)/shard_map/analysis/pallas_call | solution.py:520
  133.3 0.9 slice_bitcast_fusion.2
  134.2 1.0 slice_bitcast_fusion.1
  135.2 0.8 maximum_select_fusion.field
  136.0 4.1 %fusion.3 = bf16[3,5120,128]{2,1,0:T(8,128)(2,1)} fusion(bf16[3,16,5120]{2,1,0:T(8,128)(2,1)} %get-tuple-element.10), kind=kOutput, calls=%fused_computation.24 | convolution fusion | flops 62916608 | bytes 4423680 | tf_op jit(solution)/shard_map/dot_general | solution.py:575
  140.2 18.2 %adjoint.1 = (f32[80,8,8,128]{3,2,1,0:T(8,128)}, f32[8,8,128]{2,1,0:T(8,128)}) custom-call(s32[2]{0:T(128)} %copy-done.1, bf16[80,8,8,128]{3,2,1,0:T(8,128)(2,1)} %members.1, bf16[2,80,8,8,128]{4,3,2,1,0:T(8,128)(2,1)} %get-tuple-element.9.near, bf16[3,80,8,8,128]{4,3,2,1,0:T(8,128)(2,1)} %bitcast.30, f32[3,8,8,256]{3,2,1,0:T(8,128)} %maximum_select_fusion.field, ...), custom_call_target="tpu_custom_call" | custom-call | tf_op jit(solution)/shard_map/adjoint/pallas_call | solution.py:585
  158.3 0.6 copy.29
  (28 shorter events, 1.1 us)
Async XLA Ops:
  0.7 16.5 %copy-start.1 = (s32[2]{0:T(128)}, s32[2]{0:T(128)S(1)}, u32[]{:S(2)}) copy-start(s32[2]{0:T(128)S(1)} %add_convert_fusion.keep) | copy-start | bytes 28
  140.2 18.2 %copy-start = (f32[1,2048]{1,0:T(1,128)S(1)}, f32[1,2048]{1,0:T(1,128)}, u32[]{:S(2)}) copy-start(f32[1,2048]{1,0:T(1,128)} %get-tuple-element.14) | copy-start | bytes 24580

commit v3 on v2

--- a/solution.py
+++ b/solution.py
@@ -13,6 +13,7 @@
 BF16 = jnp.bfloat16
 F32 = jnp.float32
 MESH = pl.DeviceIdType.MESH
+CHUNKS = 4
 VMEM = pl.BlockSpec(memory_space=pltpu.VMEM)
 
 
@@ -76,6 +77,12 @@
     out[...] = total.reshape(out.shape)
 
 
+def cell_and_row(col, cells):
+    if cells & (cells - 1):
+        return col % cells, col // cells
+    return jnp.bitwise_and(col, cells - 1), jnp.right_shift(col, cells.bit_length() - 1)
+
+
 def to_slots(cols, field, out):
     levels, lat_rows, cells = field.shape
     slots = out.shape[2]
@@ -87,10 +94,11 @@
 
     def step(index, carry):
         col = cols[pl.ds(index, 1), :]
-        cell_hot = jnp.where(iota((cells, width), 0) == col % cells, 1.0, 0.0).astype(BF16)
+        cell, at_row = cell_and_row(col, cells)
+        cell_hot = jnp.where(iota((cells, width), 0) == cell, 1.0, 0.0).astype(BF16)
         product = dot(both, cell_hot)
         product = product[:count] + product[count:]
-        row = jnp.broadcast_to(col // cells, (levels, width))
+        row = jnp.broadcast_to(at_row, (levels, width))
         total = jnp.zeros((levels, width), F32)
         for r in range(lat_rows):
             total = jnp.where(row == r, product[r * levels : (r + 1) * levels], total)
@@ -98,7 +106,7 @@
             out[index * per_row + j] = total[:, j * slots : (j + 1) * slots]
         return carry
 
-    lax.fori_loop(0, cols.shape[0], step, 0)
+    lax.fori_loop(0, cols.shape[0], step, 0, unroll=4)
 
 
 def to_columns(cols, values, shape):
@@ -110,8 +118,9 @@
 
     def step(index, total):
         col = cols[pl.ds(index, 1), :]
-        cell_hot = jnp.where(iota((cells, width), 0) == col % cells, 1.0, 0.0).astype(BF16)
-        chosen = iota((lat_rows, width), 0) == col // cells
+        cell, at_row = cell_and_row(col, cells)
+        cell_hot = jnp.where(iota((cells, width), 0) == cell, 1.0, 0.0).astype(BF16)
+        chosen = iota((lat_rows, width), 0) == at_row
         value = values[index * per_row]
         if per_row > 1:
             value = jnp.concatenate(
@@ -123,7 +132,9 @@
         parts += [jnp.where(chosen, low[l : l + 1], 0.0) for l in range(levels)]
         return total + dot_nt(jnp.concatenate(parts, axis=0).astype(BF16), cell_hot)
 
-    total = lax.fori_loop(0, cols.shape[0], step, jnp.zeros((2 * count, cells), F32))
+    total = lax.fori_loop(
+        0, cols.shape[0], step, jnp.zeros((2 * count, cells), F32), unroll=4
+    )
     return (total[:count] + total[count:]).reshape(shape)
 
 
@@ -169,11 +180,76 @@
             out[spot] = total
 
 
+def banded(taps, offset):
+    total = jnp.zeros(offset.shape, F32)
+    for t in range(len(taps)):
+        total = jnp.where(offset == t, taps[t], total)
+    return total
+
+
+def block_of(ids, size, count):
+    total = jnp.zeros(ids.shape, jnp.int32)
+    for b in range(1, count):
+        total = total + jnp.where(ids >= b * size, 1, 0)
+    return total
+
+
+def make_operators(
+    height, rows, cells, lat_taps, lon_taps, lat_op, lon_op, lat_adjoint, lon_adjoint
+):
+    count = lat_taps.shape[0]
+    half = (count - 1) // 2
+    lat = [lat_taps[t] for t in range(count)]
+    lon = [lon_taps[t] for t in range(count)]
+    shape = lat_op.shape
+    blocks = shape[0] // height
+    row, col = iota(shape, 0), iota(shape, 1)
+    same = block_of(row, height, blocks) == block_of(col, height, blocks)
+    high, low = halves(jnp.where(same, banded(lat, col - row + half), 0.0))
+    lat_op[...] = dot_nt(high, high) + dot_nt(high, low) + dot_nt(low, high)
+    corr = []
+    for lag in range(-2 * half, 2 * half + 1):
+        terms = [lon[t] * lon[t - lag] for t in range(count) if 0 <= t - lag < count]
+        corr.append(functools.reduce(lambda a, b: a + b, terms))
+    shape = lon_op.shape
+    lon_op[...] = banded(corr, iota(shape, 0) - iota(shape, 1) + 2 * half - cells)
+    shape = lon_adjoint.shape
+    row = iota(shape, 0)
+    spot = jnp.where(
+        row < cells,
+        row + half,
+        jnp.where(
+            row < cells + half, row - cells, jnp.where(row < cells + 2 * half, row, 4 * cells)
+        ),
+    )
+    lon_adjoint[...] = banded(lon[::-1], spot - iota(shape, 1))
+    shape = lat_adjoint.shape
+    blocks = shape[0] // rows
+    row, col = iota(shape, 0), iota(shape, 1)
+    row_block, col_block = block_of(row, rows, blocks), block_of(col, 3 * rows, blocks)
+    offset = (col - 3 * rows * col_block) - (row - rows * row_block)
+    lat_adjoint[...] = jnp.where(row_block == col_block, banded(lat[::-1], offset), 0.0)
+
+
+def make_sides(ens, sides):
+    cells = ens.shape[3]
+    half = sides.shape[0] // 2
+    row, col = iota((2 * half, cells), 0), iota((2 * half, cells), 1)
+    pick = jnp.where(col == jnp.where(row < half, row + cells - half, row - half), 1.0, 0.0)
+    members = 8 if ens.shape[0] % 8 == 0 else 1
+    size = members * ens.shape[1] * ens.shape[2]
+    for first in range(0, ens.shape[0], members):
+        some = ens[first : first + members].reshape(size, cells)
+        at = first // members * size
+        sides[:, at : at + size] = dot_nt(pick.astype(BF16), some).astype(BF16)
+
+
 def main_kernel(
     n_lat, n_lon, iterations,
-    coef, step, ens, sides, count_row, cols, pos, level, weight, innov, prec, lat_op, lon_op,
-    departure, near, near_sides, near_held,
+    coef, step, lat_taps, lon_taps, ens, count_row, cols, pos, level, weight, innov, prec,
+    departure, near, near_sides, near_held, lat_adjoint, lon_adjoint,
     counts, whole, pushed, incoming, field, part, part_in, packed, table, held, wide, mid, hi, lo,
+    sides, lat_op, lon_op,
     ex_send, ex_recv, near_send, near_recv, side_send, side_recv, held_send, held_recv,
 ):
     lat_at, lon_at = lax.axis_index("lat"), lax.axis_index("lon")
@@ -255,6 +331,31 @@
         lo[q : q + 1, :] = place_q - jnp.sum(jnp.where(past, column, 0), axis=0, keepdims=True)
         hi[q : q + 1, :] = source * levels + level[...]
 
+    def near_chunk(chunk, begin):
+        size = ens.shape[0] // CHUNKS
+        some = pl.ds(chunk * size, size)
+        for index, turn in enumerate((1, -1)):
+            exchange_pair(
+                begin, *lat_has(n_lat, lat_at, turn),
+                src_ref=ens.at[some], dst_ref=near.at[index, some],
+                send_sem=near_send.at[index * CHUNKS + chunk],
+                recv_sem=near_recv.at[index * CHUNKS + chunk],
+                device_id=((lat_at + turn + n_lat) % n_lat, lon_at),
+            )
+
+    def side_copies(begin):
+        for up, climb in enumerate((1, 0, -1)):
+            for side, turn in enumerate((1, -1)):
+                exchange_pair(
+                    begin, *lat_has(n_lat, lat_at, climb),
+                    src_ref=sides.at[pl.ds(side * half, half)],
+                    dst_ref=near_sides.at[up, pl.ds(side * half, half)],
+                    send_sem=side_send.at[up * 2 + side], recv_sem=side_recv.at[up * 2 + side],
+                    device_id=(
+                        (lat_at + climb + n_lat) % n_lat, (lon_at + turn + n_lon) % n_lon
+                    ),
+                )
+
     number = 2
     for iteration in range(iterations):
         before = iteration - 1
@@ -262,13 +363,16 @@
             send(lambda d: held.at[d % levels], field.at[before], number)
             field[before, me] = held[me % levels]
             if iteration == 1:
+                make_sides(ens, sides)
+                make_operators(
+                    n_lat * rows, rows, cells, lat_taps, lon_taps, lat_op, lon_op,
+                    lat_adjoint, lon_adjoint,
+                )
                 wait(whole, 1)
             wait(field.at[before], number)
             if iteration == 1:
-                near_copies(
-                    n_lat, n_lon, lat_at, lon_at, half, ens, sides, near, near_sides,
-                    near_send, near_recv, side_send, side_recv, True,
-                )
+                near_chunk(0, True)
+                side_copies(True)
             covariance(
                 n_lat, n_lon, coef, whole, field.at[before], lat_op, lon_op, part, wide, mid
             )
@@ -279,11 +383,16 @@
             for g in range(1, devices // levels):
                 total = total + part_in[before, g * levels : (g + 1) * levels]
             part[0:levels] = total
+            if iteration == 1:
+                near_chunk(1, True)
             to_slots(cols, part.at[0:levels], packed)
             send(lambda d: packed.at[d], table.at[before], number + 2)
             table[before, me] = packed[me]
             wait(table.at[before], number + 2)
             number += 3
+            if iteration == 1:
+                near_chunk(2, True)
+                near_chunk(3, True)
         obs_step(
             table.at[before] if iteration > 0 else None,
             hi, lo, weight, innov, prec, departure, pushed, devices * levels, slots,
@@ -302,10 +411,9 @@
 
     held_copies(n_lat, n_lon, lat_at, lon_at, held, near_held, held_send, held_recv, True)
     near_held[1, 1] = held[...]
-    near_copies(
-        n_lat, n_lon, lat_at, lon_at, half, ens, sides, near, near_sides,
-        near_send, near_recv, side_send, side_recv, False,
-    )
+    for chunk in range(CHUNKS):
+        near_chunk(chunk, False)
+    side_copies(False)
     held_copies(n_lat, n_lon, lat_at, lon_at, held, near_held, held_send, held_recv, False)
 
 
@@ -322,30 +430,6 @@
     send = jnp.logical_and(lat_at + step >= 0, lat_at + step < n_lat)
     recv = jnp.logical_and(lat_at - step >= 0, lat_at - step < n_lat)
     return send, recv
-
-
-def near_copies(
-    n_lat, n_lon, lat_at, lon_at, half, ens, sides, near, near_sides,
-    near_send, near_recv, side_send, side_recv, begin,
-):
-    for index, step in enumerate((1, -1)):
-        has = lat_has(n_lat, lat_at, step)
-        exchange_pair(
-            begin, *has,
-            src_ref=ens, dst_ref=near.at[index],
-            send_sem=near_send.at[index], recv_sem=near_recv.at[index],
-            device_id=((lat_at + step + n_lat) % n_lat, lon_at),
-        )
-    for up, step in enumerate((1, 0, -1)):
-        has = lat_has(n_lat, lat_at, step)
-        for side, turn in enumerate((1, -1)):
-            exchange_pair(
-                begin, *has,
-                src_ref=sides.at[pl.ds(side * half, half)],
-                dst_ref=near_sides.at[up, pl.ds(side * half, half)],
-                send_sem=side_send.at[up * 2 + side], recv_sem=side_recv.at[up * 2 + side],
-                device_id=((lat_at + step + n_lat) % n_lat, (lon_at + turn + n_lon) % n_lon),
-            )
 
 
 def held_copies(n_lat, n_lon, lat_at, lon_at, held, near_held, held_send, held_recv, begin):
@@ -365,34 +449,33 @@
 def adjoint_kernel(scale, keep, members, near, edges, field, sigma, lon_op, lat_op, out, static_out):
     batch, levels, rows, cells = out.shape
     lon_high, lon_low = halves(lon_op[...])
+    lat_high, lat_low = halves(lat_op[...])
 
     def smooth(pieces, count):
-        passes = []
-        for piece in pieces:
-            high, low = halves(piece)
-            passes.append(
-                (dot(high, lon_high) + dot(high, lon_low) + dot(low, lon_high)).reshape(
-                    count, rows, cells
-                )
-            )
-        stacked = jnp.concatenate(passes, axis=1)
+        stacked = jnp.concatenate(
+            [piece.reshape(count, rows, 2 * cells) for piece in pieces], axis=1
+        )
         group = lat_op.shape[0] // rows
         results = []
         for first in range(0, count, group):
-            results.append(
-                dot3(
-                    lat_op[...],
-                    stacked[first : first + group].reshape(group * 3 * rows, cells),
-                )
+            high, low = halves(
+                stacked[first : first + group].reshape(group * 3 * rows, 2 * cells)
             )
-        return jnp.concatenate(results, axis=0)
-
+            results.append(dot(lat_high, high) + dot(lat_low, high) + dot(lat_high, low))
+        high, low = halves(jnp.concatenate(results, axis=0))
+        return dot(high, lon_high) + dot(high, lon_low) + dot(low, lon_high)
+
+    taken = edges.shape[1]
+    place = jnp.where(iota((taken, cells), 0) == iota((taken, cells), 1), 1.0, 0.0).astype(BF16)
     count = batch * levels
     pieces = []
     for part in range(3):
         values = members[...] if part == 1 else near[part // 2]
         block = values.astype(F32) * field[part, :, :, :cells][None]
-        edge = edges[part].astype(F32) * field[part, :, :, cells:][None]
+        edge = lax.dot_general(
+            edges[part], place, (((0,), (0,)), ((), ())), preferred_element_type=F32
+        ).reshape(out.shape)
+        edge = edge * field[part, :, :, cells:][None]
         piece = jnp.concatenate([block, edge], axis=-1).reshape(count * rows, 2 * cells)
         pieces.append(piece if part == 1 else jnp.where(keep[part // 2] > 0, piece, 0.0))
     out[...] = scale * smooth(pieces, count).reshape(out.shape)
@@ -401,25 +484,6 @@
     def _():
         pieces = [field[part].reshape(levels * rows, 2 * cells) for part in range(3)]
         static_out[...] = sigma[...] * smooth(pieces, levels).reshape(static_out.shape)
-
-
-def shift(block, axis, step):
-    count = lax.axis_size(axis)
-    return lax.ppermute(block, axis, [(i, (i + step) % count) for i in range(count)])
-
-
-def toeplitz(taps, shape, centre):
-    offset = iota(shape, 0) - iota(shape, 1) + centre
-    return jnp.sum(
-        jnp.where(offset[:, :, None] == iota((1, 1, taps.shape[0]), 2), taps[None, None, :], 0.0),
-        axis=2,
-    )
-
-
-def block_diagonal(matrix, count):
-    rows, cols = matrix.shape
-    tiled = jnp.tile(matrix, (count, count))
-    return jnp.where(iota(tiled.shape, 0) // rows == iota(tiled.shape, 1) // cols, tiled, 0.0)
 
 
 def divisor(count, limit):
@@ -456,55 +520,11 @@
     device_at = lat_at * n_lon + lon_at
     level_at = device_at % levels
 
-    pick = jnp.concatenate(
-        [
-            (iota((half, cells), 1) == iota((half, cells), 0) + cells - half),
-            (iota((half, cells), 1) == iota((half, cells), 0)),
-        ],
-        axis=0,
-    ).astype(BF16)
-    sides = lax.dot_general(
-        pick,
-        ensemble.reshape(-1, cells),
-        (((1,), (1,)), ((), ())),
-        preferred_element_type=BF16,
-    )
-
-    whole_lat = toeplitz(lat_taps, (n_lat * rows, n_lat * rows), half).T
-    lat_cov = jnp.dot(whole_lat, whole_lat.T, precision=lax.Precision.HIGHEST)
-    lat_cov = block_diagonal(
-        lat_cov, divisor(per_group + 1, max(1, 256 // (n_lat * rows)))
-    )
-    lon_corr = jnp.sum(
-        jnp.where(
-            iota((4 * half + 1, lon_taps.shape[0], lon_taps.shape[0]), 1)
-            - iota((4 * half + 1, lon_taps.shape[0], lon_taps.shape[0]), 2)
-            + 2 * half
-            == iota((4 * half + 1, lon_taps.shape[0], lon_taps.shape[0]), 0),
-            lon_taps[None, :, None] * lon_taps[None, None, :],
-            0.0,
-        ),
-        axis=(1, 2),
-    )
-    lon_cov = toeplitz(lon_corr, (3 * cells, cells), 2 * half - cells)
-    reverse = lon_taps[::-1]
-    extended = toeplitz(reverse, (cells + 2 * half, cells), 0)
-    lon_adjoint = jnp.concatenate(
-        [
-            extended[half : half + cells],
-            extended[:half],
-            extended[half + cells :],
-            jnp.zeros((cells - 2 * half, cells), F32),
-        ],
-        axis=0,
-    )
-    lat_adjoint = block_diagonal(
-        toeplitz(lat_taps[::-1], (rows + 2 * half, rows), 0).T, levels
-    )
-
     wide_slots = max(slots, 256)
     cols = send_cols.reshape(-1, wide_slots)
     iterations = step_len.shape[0]
+    lat_size = n_lat * rows * divisor(per_group + 1, max(1, 256 // (n_lat * rows)))
+    side_shape = (2 * half, members * levels * rows)
     later = max(1, iterations - 1)
     fields = per_group + 1
     height = n_lat * rows
@@ -517,16 +537,18 @@
     smem = pl.BlockSpec(memory_space=pltpu.SMEM)
     hbm = pl.BlockSpec(memory_space=pl.ANY)
     exchanges = 2 + iterations + 3 * (iterations - 1)
-    departure, near, near_sides, near_held = pl.pallas_call(
+    departure, near, near_sides, near_held, lat_adjoint, lon_adjoint = pl.pallas_call(
         functools.partial(main_kernel, n_lat, n_lon, iterations),
         out_shape=(
             jax.ShapeDtypeStruct((1, positions.shape[1]), F32),
             jax.ShapeDtypeStruct((2,) + ensemble.shape, BF16),
-            jax.ShapeDtypeStruct((3,) + sides.shape, BF16),
+            jax.ShapeDtypeStruct((3,) + side_shape, BF16),
             jax.ShapeDtypeStruct((3, 3, levels, rows, cells), F32),
+            jax.ShapeDtypeStruct((levels * rows, levels * 3 * rows), F32),
+            jax.ShapeDtypeStruct((2 * cells, cells), F32),
         ),
-        in_specs=[smem] * 2 + [VMEM] * 11,
-        out_specs=(VMEM, hbm, VMEM, VMEM),
+        in_specs=[smem] * 4 + [VMEM] * 8,
+        out_specs=(VMEM, hbm, VMEM, VMEM, VMEM, VMEM),
         scratch_shapes=[
             pltpu.VMEM((devices, 1, count_width), jnp.int32),
             pltpu.VMEM((devices, per_group, rows, cells), BF16),
@@ -542,10 +564,13 @@
             pltpu.VMEM((fields * height, n_lon * cells), F32),
             pltpu.VMEM(positions.shape, jnp.int32),
             pltpu.VMEM(positions.shape, jnp.int32),
+            pltpu.VMEM(side_shape, BF16),
+            pltpu.VMEM((lat_size, lat_size), F32),
+            pltpu.VMEM((3 * cells, cells), F32),
             pltpu.SemaphoreType.DMA((exchanges,)),
             pltpu.SemaphoreType.DMA((exchanges,)),
-            pltpu.SemaphoreType.DMA((2,)),
-            pltpu.SemaphoreType.DMA((2,)),
+            pltpu.SemaphoreType.DMA((2 * CHUNKS,)),
+            pltpu.SemaphoreType.DMA((2 * CHUNKS,)),
             pltpu.SemaphoreType.DMA((6,)),
             pltpu.SemaphoreType.DMA((6,)),
             pltpu.SemaphoreType.DMA((9,)),
@@ -554,9 +579,9 @@
         compiler_params=pltpu.CompilerParams(collective_id=0, has_side_effects=True),
         name="analysis",
     )(
-        coef, step_len, ensemble, sides, count_row, cols, positions,
+        coef, step_len, lat_taps, lon_taps, ensemble, count_row, cols, positions,
         obs_level.reshape(1, -1), weight, innovation.reshape(1, -1),
-        obs_precision.reshape(1, -1), lat_cov, lon_cov,
+        obs_precision.reshape(1, -1),
     )
     wide3 = jnp.concatenate(
         [
@@ -571,17 +596,13 @@
     wide3 = jnp.where(
         jnp.stack([keep[0], jnp.ones((), jnp.int32), keep[1]])[:, None, None, None] > 0, wide3, 0.0
     )
-    sides_id = (iota((2 * half, cells), 0) == iota((2 * half, cells), 1)).astype(BF16)
-    edges3 = lax.dot_general(
-        near_sides, sides_id, (((1,), (0,)), ((), ())), preferred_element_type=BF16
-    ).reshape((3,) + ensemble.shape)
     batch = divisor(members, 8)
     sigma = jnp.broadcast_to(
         (HYBRID_STATIC * static_sigma)[:, None, None], (levels, rows, cells)
     )
     own_spec = pl.BlockSpec((batch, levels, rows, cells), lambda k: (k, 0, 0, 0))
     near_spec = pl.BlockSpec((2, batch, levels, rows, cells), lambda k: (0, k, 0, 0, 0))
-    edge_spec = pl.BlockSpec((3, batch, levels, rows, cells), lambda k: (0, k, 0, 0, 0))
+    edge_spec = pl.BlockSpec((3, 2 * half, batch * levels * rows), lambda k: (0, 0, k))
     control, static = pl.pallas_call(
         functools.partial(adjoint_kernel, scale),
         grid=(members // batch,),
@@ -595,7 +616,7 @@
             pl.BlockSpec((levels, rows, cells), lambda k: (0, 0, 0)),
         ),
         name="adjoint",
-    )(keep, ensemble, near, edges3, wide3, sigma, lon_adjoint, lat_adjoint)
+    )(keep, ensemble, near, near_sides, wide3, sigma, lon_adjoint, lat_adjoint)
     return control, static, departure.reshape(1, 1, -1)
 
 

time: 159 us -> 126 us (0.79)
  Pallas kernels: 132 us -> 114 us
  matrix products: 6.79 us -> 0 us
  other arithmetic: 9.4 us -> 3.43 us
  local copies, waits for them, and re-layouts: 8.32 us -> 6.37 us
    pallas_call x1, Pallas kernels: 114 us -> 99.9 us  [per_device(): pl.pallas_call(functools.partial(main_kernel, n_lat, n_lon, iterations),...]
    dot_general x3 -> x0, matrix products: 6.79 us -> none  [the longest x1 4.15 us: per_device(): lax.dot_general(near_sides, sides_id, (((1,), (0,)), ((), ())), preferred...]
    pallas_call x1, Pallas kernels: 18.2 us -> 13.7 us  [per_device(): pl.pallas_call(functools.partial(adjoint_kernel, scale), grid=(members //...]
    reduce_sum x5 -> x0, other arithmetic: 2.54 us -> none  [the longest x4 2.41 us: toeplitz(): jnp.sum(jnp.where(offset[:, :, None] == iota((1, 1, taps.shape[0]), 2), t...]
where the time goes in v3:
time: 126 us; the launch traced here: 125 us
  Pallas kernels  114 us (90%)
  local copies, waits for them, and re-layouts  6.37 us (5%)
  other arithmetic  3.43 us (3%)
  between operations  1.99 us (2%)
    pallas_call x1, Pallas kernels, per_device(): pl.pallas_call(functools.partial(main_kernel, n_lat, n_lon, iterations),...  99.9 us
    pallas_call x1, Pallas kernels, per_device(): pl.pallas_call(functools.partial(adjoint_kernel, scale), grid=(members //...  13.7 us

profile of v3, /device:TPU:0, one launch (start us, length us, event | category | flops | bytes accessed | tf_op | source)
XLA Modules:
  0.0 125.4 jit_solution(11817842904031562640)
XLA Ops:
  0.7 0.1 add_convert_fusion.keep
  0.7 0.0 copy-start.1
  0.7 1.2 dynamic_slice.3
  3.3 0.6 pad_maximum_fusion.coef
  3.9 1.2 pad.4.count_row
  5.0 0.7 broadcast_multiply_fusion
  5.7 0.1 pad.8.clone
  5.8 0.7 fusion
  6.4 1.3 %add_compare_fusion = pred[3]{0:T(512)(128)(4,1)S(1)} fusion(s32[1]{0:T(128)} %get-tuple-element.22, s32[1]{0:T(128)} %constant.37.clone.1, s32[1]{0:T(128)} %get-tuple-element.21), kind=kLoop, calls=%fused_computation.6 | loop fusion | flops 9 | bytes 15 | tf_op jit(solution)/shard_map/gt | solution.py:597
  7.8 0.7 broadcast_in_dim.25.sigma
  8.4 99.9 %analysis.1 = (f32[1,2048]{1,0:T(1,128)}, bf16[2,80,8,8,128]{4,3,2,1,0:T(8,128)(2,1)}, bf16[3,16,5120]{2,1,0:T(8,128)(2,1)}, f32[3,3,8,8,128]{4,3,2,1,0:T(8,128)...) custom-call(f32[2]{0:T(128)} %pad_maximum_fusion.coef, f32[2]{0:T(128)} %step.1, f32[17]{0:T(128)} %lat_taps.1, f32[17]{0:T(128)} %lon_taps.1, ...), custom_call_target="tpu_custom_call" | custom-call | tf_op jit(solution)/shard_map/analysis/pallas_call | solution.py:540
  108.4 0.9 slice_bitcast_fusion.2
  109.3 1.0 slice_bitcast_fusion.1
  110.3 0.0 copy-start
  110.3 0.8 maximum_select_fusion.field
  111.1 0.0 copy-done.1
  111.1 13.7 %adjoint.1 = (f32[80,8,8,128]{3,2,1,0:T(8,128)}, f32[8,8,128]{2,1,0:T(8,128)}) custom-call(s32[2]{0:T(128)} %copy-done.1, bf16[80,8,8,128]{3,2,1,0:T(8,128)(2,1)} %members.1, bf16[2,80,8,8,128]{4,3,2,1,0:T(8,128)(2,1)} %get-tuple-element.11.near, bf16[3,16,5120]{2,1,0:T(8,128)(2,1)} %get-tuple-element.12.edges, f32[3,8,8,256]{3,2,1,0:T(8,128)} %maximum_select_fusion.field, ...), custom_call_target="tpu_custom_call" | custom-call | tf_op jit(solution)/shard_map/adjoint/pallas_call | solution.py:606
  124.8 0.0 copy-done
  124.8 0.6 copy.23
  (1 shorter events, 0.0 us)
Async XLA Ops:
  0.7 110.4 %copy-start.1 = (s32[2]{0:T(128)}, s32[2]{0:T(128)S(1)}, u32[]{:S(2)}) copy-start(s32[2]{0:T(128)S(1)} %add_convert_fusion.keep) | copy-start | bytes 28
  110.3 14.5 %copy-start = (f32[1,2048]{1,0:T(1,128)S(1)}, f32[1,2048]{1,0:T(1,128)}, u32[]{:S(2)}) copy-start(f32[1,2048]{1,0:T(1,128)} %get-tuple-element.18) | copy-start | bytes 24580
